TPU v7x, 32 devices: a whole 2x2x4 slice. The times are simulated.
32 devices in a mesh: gx: 8 (over z, core), gy: 2 (over y), vert: 2 (over x).
Axes of the slice: x: 2, y: 2, z: 4, core: 2. Of those that a mesh axis runs over, the one named last changes fastest.
Arguments:
- vectors: float32 [16, 64, 16, 128], P('vert', 'gx', 'gy'), may hold values from -6 to 6
- conductivity: float32 [64, 16, 128], P('gx', 'gy'), may hold values from 0.3 to 3
- c_points: int32 [64, 16, 16], P('gx', 'gy'), may hold values from -1 to 127, as said below
Outputs:
- interp: float32 [64, 16, 16, 128], P('gx', 'gy')
- coarse: float32 [64, 16, 9, 256], P('gx', 'gy')
Inputs may be any that keep to these rules, and one draw needn't show every extreme that they name: `c_points`: in each tile column the used slots come first, hold distinct positions in increasing order, and number at least 8; some column uses all 16 slots.
All inputs are finite; a program needn't handle non-finite values.
Results may differ from a plain program's by a relative error of at most 0.0003.
Values sent between devices are 32-bit elements; how exact they have to be, the bound alone decides.
A program may use at most 64 MiB of HBM per device.

v0:
```python
import jax
import jax.numpy as jnp
from jax import lax
from jax.sharding import PartitionSpec as P

SWEEPS = 3


ANISOTROPY = (1.0, 0.6, 0.15)
OMEGA = 0.6
SHIFT = 0.5
RIDGE = 0.1


def padded_2(block, sides, width):
    for axis, dim in sides:
        count = lax.axis_size(axis)
        forward = [(i, i + 1) for i in range(count - 1)]
        backward = [(target, source) for source, target in forward]
        low = lax.ppermute(
            lax.slice_in_dim(block, block.shape[dim] - width, None, axis=dim), axis, forward
        )
        high = lax.ppermute(lax.slice_in_dim(block, 0, width, axis=dim), axis, backward)
        block = jnp.concatenate([low, block, high], axis=dim)
    return block


def stencil_offsets():
    result = []
    for move_x in (-1, 0, 1):
        for move_y in (-1, 0, 1):
            for move_z in (-1, 0, 1):
                if move_x != 0 or move_y != 0 or move_z != 0:
                    result.append((move_x, move_y, move_z))
    return result


def coupling(move):
    weight = 1.0
    for axis_no in range(3):
        if move[axis_no] != 0:
            weight = weight * ANISOTROPY[axis_no]
    return weight


def window_of(move, shape):
    return tuple(
        (slice(1 + move[axis_no], 1 + move[axis_no] + shape[axis_no]) for axis_no in range(3))
    )


def pad_depth(array):
    return jnp.pad(array, [(0, 0)] * (array.ndim - 1) + [(1, 1)])


def operator_apply(padded, kpad):
    shape = (kpad.shape[0] - 2, kpad.shape[1] - 2, kpad.shape[2] - 2)
    interior = kpad[1:-1, 1:-1, 1:-1]
    centre = padded[:, 1:-1, 1:-1, 1:-1]
    diagonal = SHIFT * interior * interior
    nearby = jnp.zeros_like(centre)
    for move in stencil_offsets():
        window = window_of(move, shape)
        couple = coupling(move) * interior * kpad[window]
        diagonal = diagonal + couple
        nearby = nearby + couple * padded[(slice(None),) + window]
    return (diagonal * centre - nearby, diagonal, centre)


def jacobi(padded, kpad):
    image, diagonal, centre = operator_apply(padded, kpad)
    alive = diagonal > 0.0
    guarded = jnp.where(alive, diagonal, 1.0)
    return jnp.where(alive, centre - OMEGA * image / guarded, 0.0)


def onehot_of(c_points, depth):
    return (c_points[..., None] == jnp.arange(depth, dtype=jnp.int32)).astype(jnp.float32)


def gram_terms(field, onehot):
    cvals = jnp.einsum("vxyz,xyjz->vxyj", field, onehot, precision=lax.Precision.HIGHEST)
    right = jnp.einsum("vxyz,vxyj->xyjz", field, cvals, precision=lax.Precision.HIGHEST)
    gram = jnp.einsum("vxyi,vxyj->xyij", cvals, cvals, precision=lax.Precision.HIGHEST)
    return (right, gram)


def batched_solve(system, right):
    slots = system.shape[0]
    lower = [[None] * slots for row in range(slots)]
    for col in range(slots):
        total = system[col, col]
        for inner in range(col):
            total = total - lower[col][inner] * lower[col][inner]
        pivot = jnp.sqrt(total)
        lower[col][col] = pivot
        for row in range(col + 1, slots):
            total = system[row, col]
            for inner in range(col):
                total = total - lower[row][inner] * lower[col][inner]
            lower[row][col] = total / pivot
    forward = []
    for row in range(slots):
        total = right[row]
        for inner in range(row):
            total = total - lower[row][inner][:, None] * forward[inner]
        forward.append(total / lower[row][row][:, None])
    backward = [None] * slots
    for row in range(slots - 1, -1, -1):
        total = forward[row]
        for inner in range(row + 1, slots):
            total = total - lower[inner][row][:, None] * backward[inner]
        backward[row] = total / lower[row][row][:, None]
    return jnp.stack(backward, axis=0)


def solve_interp(right, gram, onehot):
    cols_x, cols_y, slots, depth = right.shape
    ridge = RIDGE * jnp.trace(gram, axis1=2, axis2=3) / slots + 1e-06
    system = gram + ridge[:, :, None, None] * jnp.eye(slots, dtype=jnp.float32)
    system_last = jnp.transpose(system.reshape(cols_x * cols_y, slots, slots), (1, 2, 0))
    right_last = jnp.transpose(right.reshape(cols_x * cols_y, slots, depth), (1, 0, 2))
    solved = batched_solve(system_last, right_last)
    weights = jnp.transpose(solved, (1, 0, 2)).reshape(cols_x, cols_y, slots, depth)
    c_row = jnp.sum(onehot, axis=2)
    return weights * (1.0 - c_row[:, :, None, :]) + onehot


def galerkin(interp, ppad, kpad):
    shape = (kpad.shape[0] - 2, kpad.shape[1] - 2, kpad.shape[2] - 2)
    interior = kpad[1:-1, 1:-1, 1:-1]
    diagonal = SHIFT * interior * interior
    for move in stencil_offsets():
        diagonal = diagonal + coupling(move) * interior * kpad[window_of(move, shape)]
    blocks = []
    slots = interp.shape[2]
    for move_x in (-1, 0, 1):
        for move_y in (-1, 0, 1):
            if move_x == 0 and move_y == 0:
                image = diagonal[:, :, None, :] * interp
            else:
                image = jnp.zeros_like(interp)
            for move_z in (-1, 0, 1):
                if move_x == 0 and move_y == 0 and (move_z == 0):
                    continue
                move = (move_x, move_y, move_z)
                window = window_of(move, shape)
                couple = coupling(move) * interior * kpad[window]
                source = ppad[window[0], window[1], :, window[2]]
                image = image - couple[:, :, None, :] * source
            block = jnp.einsum("xyiz,xyjz->xyij", interp, image, precision=lax.Precision.HIGHEST)
            blocks.append(block.reshape(shape[0], shape[1], slots * slots))
    return jnp.stack(blocks, axis=2)


def body(vectors, conductivity, c_points):
    field = vectors
    krim = padded_2(conductivity, (("gx", 0), ("gy", 1)), 1)
    kpad = pad_depth(krim)
    for turn in range(SWEEPS):
        extended = padded_2(field, (("gx", 1), ("gy", 2)), 1)
        field = jacobi(pad_depth(extended), kpad)
    onehot = onehot_of(c_points, field.shape[-1])
    whole = lax.all_gather(field, "vert", axis=0, tiled=True)
    right, gram = gram_terms(whole, onehot)
    interp = solve_interp(right, gram, onehot)
    prim = padded_2(interp, (("gx", 0), ("gy", 1)), 1)
    coarse = galerkin(interp, pad_depth(prim), kpad)
    return (interp, coarse)


def solution(mesh):
    placed = (P("vert", "gx", "gy", None), P("gx", "gy", None), P("gx", "gy", None))
    return jax.shard_map(
        body,
        mesh=mesh,
        in_specs=placed,
        out_specs=(P("gx", "gy", None, None), P("gx", "gy", None, None)),
        check_vma=False,
    )
```

profile of v0, /device:TPU:1, one launch (start us, length us, event | category | flops | bytes accessed | tf_op | source)
XLA Modules:
  0.0 124.4 jit_solution(1838056040090875284)
XLA Ops:
  1.4 4.6 %collective-permute-start = (f32[1,8,128]{2,1,0:T(8,128)S(1)}, f32[1,8,128]{2,1,0:T(8,128)S(1)}, u32[]{:S(2)}, u32[]{:S(2)}) collective-permute-start(f32[1,8,128]{2,1,0:T(8,128)S(1)} %get-tuple-element.422), channel_id=1, source_target_pairs={{0,4},{4,8},{8,12},{12,16},{16,20},{20,24},{24,28},{1,5},{5,9},{9,... | collective-permute-start | bytes 12296 | tf_op jit(solution)/shard_map/ppermute | solution.py:20
  6.0 1.9 %collective-permute-start.1 = (f32[1,8,128]{2,1,0:T(8,128)S(1)}, f32[1,8,128]{2,1,0:T(8,128)S(1)}, u32[]{:S(2)}, u32[]{:S(2)}) collective-permute-start(f32[1,8,128]{2,1,0:T(8,128)S(1)} %get-tuple-element.421), channel_id=1, source_target_pairs={{4,0},{8,4},{12,8},{16,12},{20,16},{24,20},{28,24},{5,1},{9,5},{13... | collective-permute-start | bytes 12296 | tf_op jit(solution)/shard_map/ppermute | solution.py:23
  7.9 1.1 copy.92
  9.0 1.9 %collective-permute-done.1 = f32[1,8,128]{2,1,0:T(8,128)S(1)} collective-permute-done((f32[1,8,128]{2,1,0:T(8,128)S(1)}, f32[1,8,128]{2,1,0:T(8,128)S(1)}, u32[]{:S(2)}, u32[]{:S(2)}) %collective-permute-start.1) | collective-permute-done | bytes 4128 | tf_op jit(solution)/shard_map/ppermute | solution.py:23
  10.9 0.9 fusion.243
  11.8 3.1 %collective-permute-start.2 = (f32[10,1,128]{2,1,0:T(1,128)S(1)}, f32[10,1,128]{2,1,0:T(1,128)S(1)}, u32[]{:S(2)}, u32[]{:S(2)}) collective-permute-start(f32[10,1,128]{2,1,0:T(1,128)S(1)} %get-tuple-element.416), channel_id=1, source_target_pairs={{0,2},{1,3},{4,6},{5,7},{8,10},{9,11},{12,14},{13,15},{16,18},{17,... | collective-permute-start | bytes 15368 | tf_op jit(solution)/shard_map/ppermute | solution.py:20
  15.0 1.3 %collective-permute-start.3 = (f32[10,1,128]{2,1,0:T(1,128)S(1)}, f32[10,1,128]{2,1,0:T(1,128)S(1)}, u32[]{:S(2)}, u32[]{:S(2)}) collective-permute-start(f32[10,1,128]{2,1,0:T(1,128)S(1)} %get-tuple-element.417), channel_id=1, source_target_pairs={{2,0},{3,1},{6,4},{7,5},{10,8},{11,9},{14,12},{15,13},{18,16},{19,... | collective-permute-start | bytes 15368 | tf_op jit(solution)/shard_map/ppermute | solution.py:23
  16.3 1.9 %collective-permute-start.5 = (f32[8,1,8,128]{3,0,2,1:T(8,128)S(1)}, f32[8,1,8,128]{3,0,2,1:T(8,128)S(1)}, u32[]{:S(2)}, u32[]{:S(2)}) collective-permute-start(f32[8,1,8,128]{3,0,2,1:T(8,128)S(1)} %get-tuple-element.348), channel_id=1, source_target_pairs={{4,0},{8,4},{12,8},{16,12},{20,16},{24,20},{28,24},{5,1},{9,5},{13... | collective-permute-start | bytes 98312 | tf_op jit(solution)/shard_map/ppermute | solution.py:23
  18.2 3.6 %collective-permute-start.4 = (f32[8,1,8,128]{3,0,2,1:T(8,128)S(1)}, f32[8,1,8,128]{3,0,2,1:T(8,128)S(1)}, u32[]{:S(2)}, u32[]{:S(2)}) collective-permute-start(f32[8,1,8,128]{3,0,2,1:T(8,128)S(1)} %get-tuple-element.349), channel_id=1, source_target_pairs={{0,4},{4,8},{8,12},{12,16},{16,20},{20,24},{24,28},{1,5},{5,9},{9,... | collective-permute-start | bytes 98312 | tf_op jit(solution)/shard_map/ppermute | solution.py:20
  22.0 0.9 slice_multiply_fusion.107
  23.4 4.0 %collective-permute-start.6 = (f32[8,10,1,128]{3,0,2,1:T(8,128)S(1)}, f32[8,10,1,128]{3,0,2,1:T(8,128)S(1)}, u32[]{:S(2)}, u32[]{:S(2)}) collective-permute-start(f32[8,10,1,128]{3,0,2,1:T(8,128)S(1)} %get-tuple-element.342), channel_id=1, source_target_pairs={{0,2},{1,3},{4,6},{5,7},{8,10},{9,11},{12,14},{13,15},{16,18},{17,... | collective-permute-start | bytes 122888 | tf_op jit(solution)/shard_map/ppermute | solution.py:20
  27.4 1.3 %collective-permute-start.7 = (f32[8,10,1,128]{3,0,2,1:T(8,128)S(1)}, f32[8,10,1,128]{3,0,2,1:T(8,128)S(1)}, u32[]{:S(2)}, u32[]{:S(2)}) collective-permute-start(f32[8,10,1,128]{3,0,2,1:T(8,128)S(1)} %get-tuple-element.343), channel_id=1, source_target_pairs={{2,0},{3,1},{6,4},{7,5},{10,8},{11,9},{14,12},{15,13},{18,16},{19,... | collective-permute-start | bytes 122888 | tf_op jit(solution)/shard_map/ppermute | solution.py:23
  28.7 3.4 %collective-permute-done.7 = f32[8,10,1,128]{3,0,2,1:T(8,128)S(1)} collective-permute-done((f32[8,10,1,128]{3,0,2,1:T(8,128)S(1)}, f32[8,10,1,128]{3,0,2,1:T(8,128)S(1)}, u32[]{:S(2)}, u32[]{:S(2)}) %collective-permute-start.7) | collective-permute-done | bytes 40992 | tf_op jit(solution)/shard_map/ppermute | solution.py:23
  32.4 1.4 %subtract_select_fusion = f32[8,8,8,128]{3,0,2,1:T(8,128)S(1)} fusion(f32[8,8,8,128]{3,0,2,1:T(8,128)S(1)} %copy.92, f32[8,10,10,130]{3,0,2,1:T(8,128)S(1)} %select_maximum_fusion.12, f32[8,10,1,128]{3,0,2,1:T(8,128)S(1)} %collective-permute-done.7, f32[8,10,8,128]{3,0,2,1:T(8,128)S(1)} %constant_dynamic-update-slice_fusion.3, ...), kind=kLoop, calls=%fused_computation.320 | loop fusion | flops 4259840 | bytes 6643712 | tf_op jit(solution)/shard_map/jit(_where)/select_n | solution.py:74
  33.9 5.3 %collective-permute-start.8 = (f32[8,1,8,128]{3,0,2,1:T(8,128)S(1)}, f32[8,1,8,128]{3,0,2,1:T(8,128)S(1)}, u32[]{:S(2)}, u32[]{:S(2)}) collective-permute-start(f32[8,1,8,128]{3,0,2,1:T(8,128)S(1)} %get-tuple-element.346), channel_id=1, source_target_pairs={{0,4},{4,8},{8,12},{12,16},{16,20},{20,24},{24,28},{1,5},{5,9},{9,... | collective-permute-start | bytes 98312 | tf_op jit(solution)/shard_map/ppermute | solution.py:20
  39.2 1.9 %collective-permute-start.9 = (f32[8,1,8,128]{3,0,2,1:T(8,128)S(1)}, f32[8,1,8,128]{3,0,2,1:T(8,128)S(1)}, u32[]{:S(2)}, u32[]{:S(2)}) collective-permute-start(f32[8,1,8,128]{3,0,2,1:T(8,128)S(1)} %get-tuple-element.347), channel_id=1, source_target_pairs={{4,0},{8,4},{12,8},{16,12},{20,16},{24,20},{28,24},{5,1},{9,5},{13... | collective-permute-start | bytes 98312 | tf_op jit(solution)/shard_map/ppermute | solution.py:23
  41.4 3.1 %collective-permute-done.9 = f32[8,1,8,128]{3,0,2,1:T(8,128)S(1)} collective-permute-done((f32[8,1,8,128]{3,0,2,1:T(8,128)S(1)}, f32[8,1,8,128]{3,0,2,1:T(8,128)S(1)}, u32[]{:S(2)}, u32[]{:S(2)}) %collective-permute-start.9) | collective-permute-done | bytes 32800 | tf_op jit(solution)/shard_map/ppermute | solution.py:23
  44.4 1.3 %collective-permute-start.10 = (f32[8,10,1,128]{3,0,2,1:T(8,128)S(1)}, f32[8,10,1,128]{3,0,2,1:T(8,128)S(1)}, u32[]{:S(2)}, u32[]{:S(2)}) collective-permute-start(f32[8,10,1,128]{3,0,2,1:T(8,128)S(1)} %get-tuple-element.340), channel_id=1, source_target_pairs={{0,2},{1,3},{4,6},{5,7},{8,10},{9,11},{12,14},{13,15},{16,18},{17,... | collective-permute-start | bytes 122888 | tf_op jit(solution)/shard_map/ppermute | solution.py:20
  45.8 1.3 %collective-permute-start.11 = (f32[8,10,1,128]{3,0,2,1:T(8,128)S(1)}, f32[8,10,1,128]{3,0,2,1:T(8,128)S(1)}, u32[]{:S(2)}, u32[]{:S(2)}) collective-permute-start(f32[8,10,1,128]{3,0,2,1:T(8,128)S(1)} %get-tuple-element.341), channel_id=1, source_target_pairs={{2,0},{3,1},{6,4},{7,5},{10,8},{11,9},{14,12},{15,13},{18,16},{19,... | collective-permute-start | bytes 122888 | tf_op jit(solution)/shard_map/ppermute | solution.py:23
  47.1 3.4 %collective-permute-done.11 = f32[8,10,1,128]{3,0,2,1:T(8,128)S(1)} collective-permute-done((f32[8,10,1,128]{3,0,2,1:T(8,128)S(1)}, f32[8,10,1,128]{3,0,2,1:T(8,128)S(1)}, u32[]{:S(2)}, u32[]{:S(2)}) %collective-permute-start.11) | collective-permute-done | bytes 40992 | tf_op jit(solution)/shard_map/ppermute | solution.py:23
  51.6 3.3 %collective-permute-start.12 = (f32[8,1,8,128]{3,0,2,1:T(8,128)S(1)}, f32[8,1,8,128]{3,0,2,1:T(8,128)S(1)}, u32[]{:S(2)}, u32[]{:S(2)}) collective-permute-start(f32[8,1,8,128]{3,0,2,1:T(8,128)S(1)} %get-tuple-element.344), channel_id=1, source_target_pairs={{0,4},{4,8},{8,12},{12,16},{16,20},{20,24},{24,28},{1,5},{5,9},{9,... | collective-permute-start | bytes 98312 | tf_op jit(solution)/shard_map/ppermute | solution.py:20
  55.0 1.9 %collective-permute-start.13 = (f32[8,1,8,128]{3,0,2,1:T(8,128)S(1)}, f32[8,1,8,128]{3,0,2,1:T(8,128)S(1)}, u32[]{:S(2)}, u32[]{:S(2)}) collective-permute-start(f32[8,1,8,128]{3,0,2,1:T(8,128)S(1)} %get-tuple-element.345), channel_id=1, source_target_pairs={{4,0},{8,4},{12,8},{16,12},{20,16},{24,20},{28,24},{5,1},{9,5},{13... | collective-permute-start | bytes 98312 | tf_op jit(solution)/shard_map/ppermute | solution.py:23
  56.9 3.3 %collective-permute-done.13 = f32[8,1,8,128]{3,0,2,1:T(8,128)S(1)} collective-permute-done((f32[8,1,8,128]{3,0,2,1:T(8,128)S(1)}, f32[8,1,8,128]{3,0,2,1:T(8,128)S(1)}, u32[]{:S(2)}, u32[]{:S(2)}) %collective-permute-start.13) | collective-permute-done | bytes 32800 | tf_op jit(solution)/shard_map/ppermute | solution.py:23
  60.2 1.3 %collective-permute-start.14 = (f32[8,10,1,128]{3,0,2,1:T(8,128)S(1)}, f32[8,10,1,128]{3,0,2,1:T(8,128)S(1)}, u32[]{:S(2)}, u32[]{:S(2)}) collective-permute-start(f32[8,10,1,128]{3,0,2,1:T(8,128)S(1)} %get-tuple-element.336), channel_id=1, source_target_pairs={{0,2},{1,3},{4,6},{5,7},{8,10},{9,11},{12,14},{13,15},{16,18},{17,... | collective-permute-start | bytes 122888 | tf_op jit(solution)/shard_map/ppermute | solution.py:20
  61.5 1.3 %collective-permute-start.15 = (f32[8,10,1,128]{3,0,2,1:T(8,128)S(1)}, f32[8,10,1,128]{3,0,2,1:T(8,128)S(1)}, u32[]{:S(2)}, u32[]{:S(2)}) collective-permute-start(f32[8,10,1,128]{3,0,2,1:T(8,128)S(1)} %get-tuple-element.337), channel_id=1, source_target_pairs={{2,0},{3,1},{6,4},{7,5},{10,8},{11,9},{14,12},{15,13},{18,16},{19,... | collective-permute-start | bytes 122888 | tf_op jit(solution)/shard_map/ppermute | solution.py:23
  62.8 3.4 %collective-permute-done.15 = f32[8,10,1,128]{3,0,2,1:T(8,128)S(1)} collective-permute-done((f32[8,10,1,128]{3,0,2,1:T(8,128)S(1)}, f32[8,10,1,128]{3,0,2,1:T(8,128)S(1)}, u32[]{:S(2)}, u32[]{:S(2)}) %collective-permute-start.15) | collective-permute-done | bytes 40992 | tf_op jit(solution)/shard_map/ppermute | solution.py:23
  67.4 8.7 %all_gather.3 = f32[16,8,8,128]{3,0,2,1:T(8,128)S(1)} all-gather(f32[8,8,8,128]{3,0,2,1:T(8,128)S(1)} %fusion.108), channel_id=1, replica_groups=mesh['gx'=8,'gy'=2,'vert'=2] {'vert'}, dimensions={0}, use_global_device_ids=true | all-gather | bytes 786432 | tf_op jit(solution)/shard_map/all_gather | solution.py:164
  77.3 1.1 select_reduce_fusion
  80.9 2.4 %subtract_divide_fusion.26 = (f32[64,128]{1,0:T(8,128)S(1)}, f32[64,128]{1,0:T(8,128)S(1)}, f32[64,128]{1,0:T(8,128)S(1)}, f32[64,128]{1,0:T(8,128)S(1)}, f32[64...) fusion(f32[16,64,128]{2,1,0:T(8,128)S(1)} %bitcast.1921, ...), kind=kLoop, calls=%fused_computation.596 | loop fusion | flops 3932160 | bytes 886784 | tf_op jit(solution)/shard_map/div | solution.py:113
  83.4 1.4 %constant_dynamic-update-slice_fusion.21 = f32[16,64,128]{2,1,0:T(8,128)S(1)} fusion(f32[64,128]{1,0:T(8,128)S(1)} %get-tuple-element.21, f32[64,128]{1,0:T(8,128)S(1)} %get-tuple-element.20, f32[64,128]{1,0:T(8,128)S(1)} %get-tuple-element.19, f32[64,128]{1,0:T(8,128)S(1)} %get-tuple-element.18, f32[64,128]{1,0:T(8,128)S(1)} %get-tuple-element.25, ...), kind=kLoop, calls=%fused_computation.359 | loop fusion | flops 2473983 | bytes 652800
  84.8 2.4 %constant_dynamic-update-slice_fusion.18 = (f32[16,64,128]{2,1,0:T(8,128)S(1)}, f32[1,64,128]{2,1,0:T(8,128)S(1)}, f32[1,64,128]{2,1,0:T(8,128)S(1)}, f32[1,64,1...) fusion(f32[16,64,128]{2,1,0:T(8,128)S(1)} %constant_dynamic-upd, ...), kind=kLoop, calls=%fused_computation.356 | loop fusion | flops 3350528 | bytes 1015808
  88.2 3.9 %collective-permute-start.16 = (f32[1,8,16,128]{3,2,1,0:T(8,128)S(1)}, f32[1,8,16,128]{3,2,1,0:T(8,128)S(1)}, u32[]{:S(2)}, u32[]{:S(2)}) collective-permute-start(f32[1,8,16,128]{3,2,1,0:T(8,128)S(1)} %get-tuple-element.332), channel_id=1, source_target_pairs={{0,4},{4,8},{8,12},{12,16},{16,20},{20,24},{24,28},{1,5},{5,9},{9,... | collective-permute-start | bytes 196616 | tf_op jit(solution)/shard_map/ppermute | solution.py:20
  92.2 1.9 %collective-permute-start.17 = (f32[1,8,16,128]{3,2,1,0:T(8,128)S(1)}, f32[1,8,16,128]{3,2,1,0:T(8,128)S(1)}, u32[]{:S(2)}, u32[]{:S(2)}) collective-permute-start(f32[1,8,16,128]{3,2,1,0:T(8,128)S(1)} %get-tuple-element.333), channel_id=1, source_target_pairs={{4,0},{8,4},{12,8},{16,12},{20,16},{24,20},{28,24},{5,1},{9,5},{13... | collective-permute-start | bytes 196616 | tf_op jit(solution)/shard_map/ppermute | solution.py:23
  94.1 3.6 %collective-permute-done.17 = f32[1,8,16,128]{3,2,1,0:T(8,128)S(1)} collective-permute-done((f32[1,8,16,128]{3,2,1,0:T(8,128)S(1)}, f32[1,8,16,128]{3,2,1,0:T(8,128)S(1)}, u32[]{:S(2)}, u32[]{:S(2)}) %collective-permute-start.17) | collective-permute-done | bytes 65568 | tf_op jit(solution)/shard_map/ppermute | solution.py:23
  97.8 1.6 %collective-permute-start.18 = (f32[10,1,16,128]{3,2,1,0:T(8,128)S(1)}, f32[10,1,16,128]{3,2,1,0:T(8,128)S(1)}, u32[]{:S(2)}, u32[]{:S(2)}) collective-permute-start(f32[10,1,16,128]{3,2,1,0:T(8,128)S(1)} %get-tuple-element.330), channel_id=1, source_target_pairs={{0,2},{1,3},{4,6},{5,7},{8,10},{9,11},{12,14},{13,15},{16,18},{17,... | collective-permute-start | bytes 245768 | tf_op jit(solution)/shard_map/ppermute | solution.py:20
  99.4 1.5 %collective-permute-start.19 = (f32[10,1,16,128]{3,2,1,0:T(8,128)S(1)}, f32[10,1,16,128]{3,2,1,0:T(8,128)S(1)}, u32[]{:S(2)}, u32[]{:S(2)}) collective-permute-start(f32[10,1,16,128]{3,2,1,0:T(8,128)S(1)} %get-tuple-element.331), channel_id=1, source_target_pairs={{2,0},{3,1},{6,4},{7,5},{10,8},{11,9},{14,12},{15,13},{18,16},{19,... | collective-permute-start | bytes 245768 | tf_op jit(solution)/shard_map/ppermute | solution.py:23
  100.9 3.7 %collective-permute-done.19 = f32[10,1,16,128]{3,2,1,0:T(8,128)S(1)} collective-permute-done((f32[10,1,16,128]{3,2,1,0:T(8,128)S(1)}, f32[10,1,16,128]{3,2,1,0:T(8,128)S(1)}, u32[]{:S(2)}, u32[]{:S(2)}) %collective-permute-start.19) | collective-permute-done | bytes 81952 | tf_op jit(solution)/shard_map/ppermute | solution.py:23
  105.5 1.1 fusion.26
  106.6 1.9 %fusion.45 = f32[8,8,16,16]{3,2,1,0:T(8,128)} fusion(f32[8,8,16,128]{3,2,1,0:T(8,128)S(1)} %convert_add_fusion, f32[10,10,16,130]{3,2,1,0:T(8,128)S(1)} %select_maximum_fusion, f32[10,9,16,128]{3,2,1,0:T(8,128)S(1)} %get-tuple-element.328, f32[8,8,128]{2,1,0:T(8,128)S(1)} %get-tuple-element.362, f32[8,8,128]{2,1,0:T(8,128)S(1)} %copy-done.10, ...), kind=kOutput, calls=%fused_computation.69 | convolution fusion | flops 25952256 | bytes 2260992 | tf_op jit(solution)/shard_map/xyiz,xyjz->xyij/dot_general | solution.py:151
  108.5 1.9 %fusion.3 = f32[8,8,16,16]{3,2,1,0:T(8,128)} fusion(f32[8,8,16,128]{3,2,1,0:T(8,128)S(1)} %convert_add_fusion, f32[10,10,16,130]{3,2,1,0:T(8,128)S(1)} %select_maximum_fusion, f32[10,9,16,128]{3,2,1,0:T(8,128)S(1)} %get-tuple-element.328, f32[8,8,128]{2,1,0:T(8,128)S(1)} %get-tuple-element.327, f32[8,8,128]{2,1,0:T(8,128)S(1)} %get-tuple-element.320, ...), kind=kOutput, calls=%fused_computation.27 | convolution fusion | flops 25952256 | bytes 2260992 | tf_op jit(solution)/shard_map/xyiz,xyjz->xyij/dot_general | solution.py:151
  110.4 1.9 %fusion.38 = f32[8,8,16,16]{3,2,1,0:T(8,128)} fusion(f32[8,8,16,128]{3,2,1,0:T(8,128)S(1)} %convert_add_fusion, f32[10,10,16,130]{3,2,1,0:T(8,128)S(1)} %select_maximum_fusion, f32[10,9,16,128]{3,2,1,0:T(8,128)S(1)} %get-tuple-element.329, f32[8,8,128]{2,1,0:T(8,128)S(1)} %get-tuple-element.360, f32[8,8,128]{2,1,0:T(8,128)S(1)} %copy-done.8, ...), kind=kOutput, calls=%fused_computation.62 | convolution fusion | flops 25952256 | bytes 2260992 | tf_op jit(solution)/shard_map/xyiz,xyjz->xyij/dot_general | solution.py:151
  112.2 1.9 %fusion.19 = f32[8,8,16,16]{3,2,1,0:T(8,128)} fusion(f32[8,8,16,128]{3,2,1,0:T(8,128)S(1)} %convert_add_fusion, f32[10,10,16,130]{3,2,1,0:T(8,128)S(1)} %select_maximum_fusion, f32[10,9,16,128]{3,2,1,0:T(8,128)S(1)} %get-tuple-element.329, f32[8,8,128]{2,1,0:T(8,128)S(1)} %get-tuple-element.354, f32[8,8,128]{2,1,0:T(8,128)S(1)} %get-tuple-element.326, ...), kind=kOutput, calls=%fused_computation.43 | convolution fusion | flops 25952256 | bytes 2260992 | tf_op jit(solution)/shard_map/xyiz,xyjz->xyij/dot_general | solution.py:151
  114.1 1.9 %fusion.61 = f32[8,8,16,16]{3,2,1,0:T(8,128)} fusion(f32[8,8,16,128]{3,2,1,0:T(8,128)S(1)} %convert_add_fusion, f32[10,10,16,130]{3,2,1,0:T(8,128)S(1)} %select_maximum_fusion, f32[10,9,16,128]{3,2,1,0:T(8,128)S(1)} %get-tuple-element.329, f32[8,8,128]{2,1,0:T(8,128)S(1)} %get-tuple-element.366, f32[8,8,128]{2,1,0:T(8,128)S(1)} %get-tuple-element.322, ...), kind=kOutput, calls=%fused_computation.85 | convolution fusion | flops 25952256 | bytes 2260992 | tf_op jit(solution)/shard_map/xyiz,xyjz->xyij/dot_general | solution.py:151
  116.0 1.9 %fusion.33 = f32[8,8,16,16]{3,2,1,0:T(8,128)} fusion(f32[8,8,16,128]{3,2,1,0:T(8,128)S(1)} %convert_add_fusion, f32[10,10,16,130]{3,2,1,0:T(8,128)S(1)} %select_maximum_fusion, f32[8,8,128]{2,1,0:T(8,128)S(1)} %get-tuple-element.358, f32[8,8,128]{2,1,0:T(8,128)S(1)} %get-tuple-element.359, f32[8,8,128]{2,1,0:T(8,128)S(1)} %get-tuple-element.414), kind=kOutput, calls=%fused_computation.57 | convolution fusion | flops 25821184 | bytes 2260992 | tf_op jit(solution)/shard_map/xyiz,xyjz->xyij/dot_general | solution.py:151
  117.9 1.1 fusion.52
  119.2 1.1 fusion.10
  120.6 1.4 %stack_reshape.30 = f32[8,8,1,256]{3,1,0,2:T(8,128)S(1)} reshape(f32[8,8,16,16]{3,2,1,0:T(8,128)} %fusion.38) | data formatting | bytes 131072 | tf_op jit(solution)/shard_map/stack;reshape | solution.py:153
  123.6 0.8 copy-done.15
  (147 shorter events, 11.4 us)
Async XLA Ops:
  0.6 22.3 %copy-start.13 = (f32[8,8,128]{2,1,0:T(8,128)S(1)}, f32[8,8,128]{2,1,0:T(8,128)}, u32[]{:S(2)}) copy-start(f32[8,8,128]{2,1,0:T(8,128)} %param.4) | copy-start | bytes 98308
  0.6 22.5 %copy-start.6 = (f32[8,8,8,128]{3,2,1,0:T(8,128)S(1)}, f32[8,8,8,128]{3,2,1,0:T(8,128)}, u32[]{:S(2)}) copy-start(f32[8,8,8,128]{3,2,1,0:T(8,128)} %param.3) | copy-start | bytes 786436
  1.4 7.6 %collective-permute-start = (f32[1,8,128]{2,1,0:T(8,128)S(1)}, f32[1,8,128]{2,1,0:T(8,128)S(1)}, u32[]{:S(2)}, u32[]{:S(2)}) collective-permute-start(f32[1,8,128]{2,1,0:T(8,128)S(1)} %get-tuple-element.422), channel_id=1, source_target_pairs={{0,4},{4,8},{8,12},{12,16},{16,20},{20,24},{24,28},{1,5},{5,9},{9,... | collective-permute-start | bytes 12296 | tf_op jit(solution)/shard_map/ppermute | solution.py:20
  6.0 4.9 %collective-permute-start.1 = (f32[1,8,128]{2,1,0:T(8,128)S(1)}, f32[1,8,128]{2,1,0:T(8,128)S(1)}, u32[]{:S(2)}, u32[]{:S(2)}) collective-permute-start(f32[1,8,128]{2,1,0:T(8,128)S(1)} %get-tuple-element.421), channel_id=1, source_target_pairs={{4,0},{8,4},{12,8},{16,12},{20,16},{24,20},{28,24},{5,1},{9,5},{13... | collective-permute-start | bytes 12296 | tf_op jit(solution)/shard_map/ppermute | solution.py:23
  11.8 10.0 %collective-permute-start.2 = (f32[10,1,128]{2,1,0:T(1,128)S(1)}, f32[10,1,128]{2,1,0:T(1,128)S(1)}, u32[]{:S(2)}, u32[]{:S(2)}) collective-permute-start(f32[10,1,128]{2,1,0:T(1,128)S(1)} %get-tuple-element.416), channel_id=1, source_target_pairs={{0,2},{1,3},{4,6},{5,7},{8,10},{9,11},{12,14},{13,15},{16,18},{17,... | collective-permute-start | bytes 15368 | tf_op jit(solution)/shard_map/ppermute | solution.py:20
  15.0 6.9 %collective-permute-start.3 = (f32[10,1,128]{2,1,0:T(1,128)S(1)}, f32[10,1,128]{2,1,0:T(1,128)S(1)}, u32[]{:S(2)}, u32[]{:S(2)}) collective-permute-start(f32[10,1,128]{2,1,0:T(1,128)S(1)} %get-tuple-element.417), channel_id=1, source_target_pairs={{2,0},{3,1},{6,4},{7,5},{10,8},{11,9},{14,12},{15,13},{18,16},{19,... | collective-permute-start | bytes 15368 | tf_op jit(solution)/shard_map/ppermute | solution.py:23
  16.3 7.1 %collective-permute-start.5 = (f32[8,1,8,128]{3,0,2,1:T(8,128)S(1)}, f32[8,1,8,128]{3,0,2,1:T(8,128)S(1)}, u32[]{:S(2)}, u32[]{:S(2)}) collective-permute-start(f32[8,1,8,128]{3,0,2,1:T(8,128)S(1)} %get-tuple-element.348), channel_id=1, source_target_pairs={{4,0},{8,4},{12,8},{16,12},{20,16},{24,20},{28,24},{5,1},{9,5},{13... | collective-permute-start | bytes 98312 | tf_op jit(solution)/shard_map/ppermute | solution.py:23
  18.2 5.0 %collective-permute-start.4 = (f32[8,1,8,128]{3,0,2,1:T(8,128)S(1)}, f32[8,1,8,128]{3,0,2,1:T(8,128)S(1)}, u32[]{:S(2)}, u32[]{:S(2)}) collective-permute-start(f32[8,1,8,128]{3,0,2,1:T(8,128)S(1)} %get-tuple-element.349), channel_id=1, source_target_pairs={{0,4},{4,8},{8,12},{12,16},{16,20},{20,24},{24,28},{1,5},{5,9},{9,... | collective-permute-start | bytes 98312 | tf_op jit(solution)/shard_map/ppermute | solution.py:20
  23.1 43.5 %copy-start.7 = (f32[8,8,128]{2,1,0:T(8,128)}, f32[8,8,128]{2,1,0:T(8,128)S(1)}, u32[]{:S(2)}) copy-start(f32[8,8,128]{2,1,0:T(8,128)S(1)} %get-tuple-element.324) | copy-start | bytes 98308
  23.1 43.5 %copy-start.9 = (f32[8,8,128]{2,1,0:T(8,128)}, f32[8,8,128]{2,1,0:T(8,128)S(1)}, u32[]{:S(2)}) copy-start(f32[8,8,128]{2,1,0:T(8,128)S(1)} %get-tuple-element.323) | copy-start | bytes 98308
  23.1 43.5 %copy-start.11 = (f32[8,8,128]{2,1,0:T(8,128)}, f32[8,8,128]{2,1,0:T(8,128)S(1)}, u32[]{:S(2)}) copy-start(f32[8,8,128]{2,1,0:T(8,128)S(1)} %get-tuple-element.325) | copy-start | bytes 98308
  23.4 5.3 %collective-permute-start.6 = (f32[8,10,1,128]{3,0,2,1:T(8,128)S(1)}, f32[8,10,1,128]{3,0,2,1:T(8,128)S(1)}, u32[]{:S(2)}, u32[]{:S(2)}) collective-permute-start(f32[8,10,1,128]{3,0,2,1:T(8,128)S(1)} %get-tuple-element.342), channel_id=1, source_target_pairs={{0,2},{1,3},{4,6},{5,7},{8,10},{9,11},{12,14},{13,15},{16,18},{17,... | collective-permute-start | bytes 122888 | tf_op jit(solution)/shard_map/ppermute | solution.py:20
  27.4 4.7 %collective-permute-start.7 = (f32[8,10,1,128]{3,0,2,1:T(8,128)S(1)}, f32[8,10,1,128]{3,0,2,1:T(8,128)S(1)}, u32[]{:S(2)}, u32[]{:S(2)}) collective-permute-start(f32[8,10,1,128]{3,0,2,1:T(8,128)S(1)} %get-tuple-element.343), channel_id=1, source_target_pairs={{2,0},{3,1},{6,4},{7,5},{10,8},{11,9},{14,12},{15,13},{18,16},{19,... | collective-permute-start | bytes 122888 | tf_op jit(solution)/shard_map/ppermute | solution.py:23
  32.4 8.7 %copy-start.14 = (s32[8,8,16]{2,1,0:T(8,128)S(1)}, s32[8,8,16]{2,1,0:T(8,128)}, u32[]{:S(2)}) copy-start(s32[8,8,16]{2,1,0:T(8,128)} %param.5) | copy-start | bytes 12292
  33.9 7.5 %collective-permute-start.8 = (f32[8,1,8,128]{3,0,2,1:T(8,128)S(1)}, f32[8,1,8,128]{3,0,2,1:T(8,128)S(1)}, u32[]{:S(2)}, u32[]{:S(2)}) collective-permute-start(f32[8,1,8,128]{3,0,2,1:T(8,128)S(1)} %get-tuple-element.346), channel_id=1, source_target_pairs={{0,4},{4,8},{8,12},{12,16},{16,20},{20,24},{24,28},{1,5},{5,9},{9,... | collective-permute-start | bytes 98312 | tf_op jit(solution)/shard_map/ppermute | solution.py:20
  39.2 5.2 %collective-permute-start.9 = (f32[8,1,8,128]{3,0,2,1:T(8,128)S(1)}, f32[8,1,8,128]{3,0,2,1:T(8,128)S(1)}, u32[]{:S(2)}, u32[]{:S(2)}) collective-permute-start(f32[8,1,8,128]{3,0,2,1:T(8,128)S(1)} %get-tuple-element.347), channel_id=1, source_target_pairs={{4,0},{8,4},{12,8},{16,12},{20,16},{24,20},{28,24},{5,1},{9,5},{13... | collective-permute-start | bytes 98312 | tf_op jit(solution)/shard_map/ppermute | solution.py:23
  44.4 2.6 %collective-permute-start.10 = (f32[8,10,1,128]{3,0,2,1:T(8,128)S(1)}, f32[8,10,1,128]{3,0,2,1:T(8,128)S(1)}, u32[]{:S(2)}, u32[]{:S(2)}) collective-permute-start(f32[8,10,1,128]{3,0,2,1:T(8,128)S(1)} %get-tuple-element.340), channel_id=1, source_target_pairs={{0,2},{1,3},{4,6},{5,7},{8,10},{9,11},{12,14},{13,15},{16,18},{17,... | collective-permute-start | bytes 122888 | tf_op jit(solution)/shard_map/ppermute | solution.py:20
  45.8 4.7 %collective-permute-start.11 = (f32[8,10,1,128]{3,0,2,1:T(8,128)S(1)}, f32[8,10,1,128]{3,0,2,1:T(8,128)S(1)}, u32[]{:S(2)}, u32[]{:S(2)}) collective-permute-start(f32[8,10,1,128]{3,0,2,1:T(8,128)S(1)} %get-tuple-element.341), channel_id=1, source_target_pairs={{2,0},{3,1},{6,4},{7,5},{10,8},{11,9},{14,12},{15,13},{18,16},{19,... | collective-permute-start | bytes 122888 | tf_op jit(solution)/shard_map/ppermute | solution.py:23
  51.6 5.3 %collective-permute-start.12 = (f32[8,1,8,128]{3,0,2,1:T(8,128)S(1)}, f32[8,1,8,128]{3,0,2,1:T(8,128)S(1)}, u32[]{:S(2)}, u32[]{:S(2)}) collective-permute-start(f32[8,1,8,128]{3,0,2,1:T(8,128)S(1)} %get-tuple-element.344), channel_id=1, source_target_pairs={{0,4},{4,8},{8,12},{12,16},{16,20},{20,24},{24,28},{1,5},{5,9},{9,... | collective-permute-start | bytes 98312 | tf_op jit(solution)/shard_map/ppermute | solution.py:20
  55.0 5.2 %collective-permute-start.13 = (f32[8,1,8,128]{3,0,2,1:T(8,128)S(1)}, f32[8,1,8,128]{3,0,2,1:T(8,128)S(1)}, u32[]{:S(2)}, u32[]{:S(2)}) collective-permute-start(f32[8,1,8,128]{3,0,2,1:T(8,128)S(1)} %get-tuple-element.345), channel_id=1, source_target_pairs={{4,0},{8,4},{12,8},{16,12},{20,16},{24,20},{28,24},{5,1},{9,5},{13... | collective-permute-start | bytes 98312 | tf_op jit(solution)/shard_map/ppermute | solution.py:23
  60.2 2.6 %collective-permute-start.14 = (f32[8,10,1,128]{3,0,2,1:T(8,128)S(1)}, f32[8,10,1,128]{3,0,2,1:T(8,128)S(1)}, u32[]{:S(2)}, u32[]{:S(2)}) collective-permute-start(f32[8,10,1,128]{3,0,2,1:T(8,128)S(1)} %get-tuple-element.336), channel_id=1, source_target_pairs={{0,2},{1,3},{4,6},{5,7},{8,10},{9,11},{12,14},{13,15},{16,18},{17,... | collective-permute-start | bytes 122888 | tf_op jit(solution)/shard_map/ppermute | solution.py:20
  61.5 4.7 %collective-permute-start.15 = (f32[8,10,1,128]{3,0,2,1:T(8,128)S(1)}, f32[8,10,1,128]{3,0,2,1:T(8,128)S(1)}, u32[]{:S(2)}, u32[]{:S(2)}) collective-permute-start(f32[8,10,1,128]{3,0,2,1:T(8,128)S(1)} %get-tuple-element.337), channel_id=1, source_target_pairs={{2,0},{3,1},{6,4},{7,5},{10,8},{11,9},{14,12},{15,13},{18,16},{19,... | collective-permute-start | bytes 122888 | tf_op jit(solution)/shard_map/ppermute | solution.py:23
  88.2 31.0 %copy-start = (f32[8,8,16,128]{3,2,1,0:T(8,128)}, f32[8,8,16,128]{3,2,1,0:T(8,128)S(1)}, u32[]{:S(2)}) copy-start(f32[8,8,16,128]{3,2,1,0:T(8,128)S(1)} %convert_add_fusion) | copy-start | bytes 1572868
  88.2 5.9 %collective-permute-start.16 = (f32[1,8,16,128]{3,2,1,0:T(8,128)S(1)}, f32[1,8,16,128]{3,2,1,0:T(8,128)S(1)}, u32[]{:S(2)}, u32[]{:S(2)}) collective-permute-start(f32[1,8,16,128]{3,2,1,0:T(8,128)S(1)} %get-tuple-element.332), channel_id=1, source_target_pairs={{0,4},{4,8},{8,12},{12,16},{16,20},{20,24},{24,28},{1,5},{5,9},{9,... | collective-permute-start | bytes 196616 | tf_op jit(solution)/shard_map/ppermute | solution.py:20
  92.2 5.6 %collective-permute-start.17 = (f32[1,8,16,128]{3,2,1,0:T(8,128)S(1)}, f32[1,8,16,128]{3,2,1,0:T(8,128)S(1)}, u32[]{:S(2)}, u32[]{:S(2)}) collective-permute-start(f32[1,8,16,128]{3,2,1,0:T(8,128)S(1)} %get-tuple-element.333), channel_id=1, source_target_pairs={{4,0},{8,4},{12,8},{16,12},{20,16},{24,20},{28,24},{5,1},{9,5},{13... | collective-permute-start | bytes 196616 | tf_op jit(solution)/shard_map/ppermute | solution.py:23
  97.8 3.2 %collective-permute-start.18 = (f32[10,1,16,128]{3,2,1,0:T(8,128)S(1)}, f32[10,1,16,128]{3,2,1,0:T(8,128)S(1)}, u32[]{:S(2)}, u32[]{:S(2)}) collective-permute-start(f32[10,1,16,128]{3,2,1,0:T(8,128)S(1)} %get-tuple-element.330), channel_id=1, source_target_pairs={{0,2},{1,3},{4,6},{5,7},{8,10},{9,11},{12,14},{13,15},{16,18},{17,... | collective-permute-start | bytes 245768 | tf_op jit(solution)/shard_map/ppermute | solution.py:20
  99.4 5.2 %collective-permute-start.19 = (f32[10,1,16,128]{3,2,1,0:T(8,128)S(1)}, f32[10,1,16,128]{3,2,1,0:T(8,128)S(1)}, u32[]{:S(2)}, u32[]{:S(2)}) collective-permute-start(f32[10,1,16,128]{3,2,1,0:T(8,128)S(1)} %get-tuple-element.331), channel_id=1, source_target_pairs={{2,0},{3,1},{6,4},{7,5},{10,8},{11,9},{14,12},{15,13},{18,16},{19,... | collective-permute-start | bytes 245768 | tf_op jit(solution)/shard_map/ppermute | solution.py:23
  104.7 0.8 copy-start.12
  105.2 1.3 %copy-start.10 = (f32[8,8,128]{2,1,0:T(8,128)S(1)}, f32[8,8,128]{2,1,0:T(8,128)}, u32[]{:S(2)}) copy-start(f32[8,8,128]{2,1,0:T(8,128)} %copy-done.9) | copy-start | bytes 98308
  108.5 1.9 %copy-start.8 = (f32[8,8,128]{2,1,0:T(8,128)S(1)}, f32[8,8,128]{2,1,0:T(8,128)}, u32[]{:S(2)}) copy-start(f32[8,8,128]{2,1,0:T(8,128)} %copy-done.7) | copy-start | bytes 98308
  120.3 1.9 %copy-start.1 = (f32[8,8,16,16]{3,2,1,0:T(8,128)S(1)}, f32[8,8,16,16]{3,2,1,0:T(8,128)}, u32[]{:S(2)}) copy-start(f32[8,8,16,16]{3,2,1,0:T(8,128)} %fusion.45) | copy-start | bytes 196612
  120.3 2.2 %copy-start.2 = (f32[8,8,16,16]{3,2,1,0:T(8,128)S(1)}, f32[8,8,16,16]{3,2,1,0:T(8,128)}, u32[]{:S(2)}) copy-start(f32[8,8,16,16]{3,2,1,0:T(8,128)} %fusion.3) | copy-start | bytes 196612
  120.3 2.4 %copy-start.3 = (f32[8,8,16,16]{3,2,1,0:T(8,128)S(1)}, f32[8,8,16,16]{3,2,1,0:T(8,128)}, u32[]{:S(2)}) copy-start(f32[8,8,16,16]{3,2,1,0:T(8,128)} %fusion.19) | copy-start | bytes 196612
  120.5 2.4 %copy-start.5 = (f32[8,8,16,16]{3,2,1,0:T(8,128)S(1)}, f32[8,8,16,16]{3,2,1,0:T(8,128)}, u32[]{:S(2)}) copy-start(f32[8,8,16,16]{3,2,1,0:T(8,128)} %fusion.33) | copy-start | bytes 196612
  120.5 2.6 %copy-start.4 = (f32[8,8,16,16]{3,2,1,0:T(8,128)S(1)}, f32[8,8,16,16]{3,2,1,0:T(8,128)}, u32[]{:S(2)}) copy-start(f32[8,8,16,16]{3,2,1,0:T(8,128)} %fusion.61) | copy-start | bytes 196612
  123.6 0.8 copy-start.15
where the time goes:
time: 125 us; the launch traced here: 124 us
  starting transfers between devices  48.5 us (39%)
  waiting for transfers between devices  25.8 us (21%)
  matrix products  16.8 us (13%)
  other arithmetic  15.8 us (13%)
  blocking collectives  8.71 us (7%)
  local copies, waits for them, and re-layouts  7.09 us (6%)
  between operations  1.71 us (1%)
    ppermute x10, starting transfers between devices, padded_2(): lax.ppermute(lax.slice_in_dim(block, block.shape[dim] - width, None, axis...  32.2 us
    ppermute x10, waiting for transfers between devices, padded_2(): lax.ppermute(lax.slice_in_dim(block, 0, width, axis=dim), axis, backward)  25.8 us
    ppermute x10, starting transfers between devices, padded_2(): lax.ppermute(lax.slice_in_dim(block, 0, width, axis=dim), axis, backward)  16.3 us
    dot_general x9, matrix products, galerkin(): jnp.einsum('xyiz,xyjz->xyij', interp, image, precision=lax.Precision.HIGH...  14.5 us
    all_gather x1, blocking collectives, body(): whole = lax.all_gather(field, 'vert', axis=0, tiled=True)  8.71 us
    unnamed x5, other arithmetic  4.28 us
    another operation x10, local copies, waits for them, and re-layouts, galerkin(): return jnp.stack(blocks, axis=2)  3.34 us
    select_n x3, other arithmetic, jacobi(): return jnp.where(alive, centre - OMEGA * image / guarded, 0.0)  2.89 us
  transfers between devices with their start and end apart: 20, of which 8 were waited for; matrix products, arithmetic and copies ran while one was open for 2% of the time, Pallas kernels for 0%

commit v1 on v0

v1 whole, which is shorter than its diff:
```python
import functools

import jax
import jax.numpy as jnp
from jax import lax
from jax.experimental import pallas as pl
from jax.experimental.pallas import tpu as pltpu
from jax.sharding import PartitionSpec as P

SWEEPS = 3
ANISOTROPY = (1.0, 0.6, 0.15)
OMEGA = 0.6
SHIFT = 0.5
RIDGE = 0.1
HALO = SWEEPS + 1
GROUP = 8
MESH = pl.DeviceIdType.MESH
F32 = jnp.float32
BF16 = jnp.bfloat16


def smear_z(x):
    axis = x.ndim - 1
    depth = x.shape[axis]
    lane = lax.broadcasted_iota(jnp.int32, x.shape, axis)
    below = jnp.where(lane == 0, 0.0, pltpu.roll(x, 1, axis))
    above = jnp.where(lane == depth - 1, 0.0, pltpu.roll(x, depth - 1, axis))
    return x + ANISOTROPY[2] * (below + above)


def smear_xy(ref, row, col, pick):
    return pick(ref, row, col) + ANISOTROPY[0] * (pick(ref, row - 1, col) + pick(ref, row + 1, col))


def smear_row(ref, row, first, last, pick):
    across = {col: smear_xy(ref, row, col, pick) for col in range(first - 1, last + 1)}
    return [
        smear_z(across[col] + ANISOTROPY[1] * (across[col - 1] + across[col + 1]))
        for col in range(first, last)
    ]


def span(move, size):
    if move == 0:
        return pl.ds(0, size), pl.ds(HALO, size)
    if move > 0:
        return pl.ds(size - HALO, HALO), pl.ds(0, HALO)
    return pl.ds(0, HALO), pl.ds(size + HALO, HALO)


def hole(move, size):
    if move == 0:
        return pl.ds(HALO, size)
    return pl.ds(size + HALO, HALO) if move > 0 else pl.ds(0, HALO)


def smooth_kernel(
    nx, ny, nv, v_ref, aux_ref, out_ref, auxe_ref,
    one, two, gain, vsend, vrecv, asend, arecv, fsend, frecv,
):
    size_x, size_y, vecs, depth = v_ref.shape
    wide_x, wide_y = size_x + 2 * HALO, size_y + 2 * HALO
    gx, gy, gv = lax.axis_index("gx"), lax.axis_index("gy"), lax.axis_index("vert")
    moves = [(mx, my) for mx in (-1, 0, 1) for my in (-1, 0, 1) if (mx, my) != (0, 0)]

    def inside(mx, my):
        ok_x = jnp.logical_and(gx + mx >= 0, gx + mx < nx)
        ok_y = jnp.logical_and(gy + my >= 0, gy + my < ny)
        return jnp.logical_and(ok_x, ok_y)

    barrier = pltpu.get_barrier_semaphore()
    total = jnp.int32(nv - 1)
    for mx, my in moves:
        here = inside(mx, my)

        @pl.when(here)
        def _():
            pl.semaphore_signal(
                barrier, inc=1, device_id=(gx + mx, gy + my, gv), device_id_type=MESH
            )

        total = total + here.astype(jnp.int32)
    for step in range(1, nv):
        pl.semaphore_signal(
            barrier, inc=1, device_id=(gx, gy, lax.rem(gv + step, nv)), device_id_type=MESH
        )
    pl.semaphore_wait(barrier, total)

    def copies(no, mx, my):
        from_x, to_x = span(mx, size_x)
        from_y, to_y = span(my, size_y)
        target = (gx + mx, gy + my, gv)
        return (
            pltpu.make_async_remote_copy(
                src_ref=aux_ref.at[from_x, from_y], dst_ref=auxe_ref.at[to_x, to_y],
                send_sem=asend.at[no], recv_sem=arecv.at[no],
                device_id=target, device_id_type=MESH,
            ),
            pltpu.make_async_remote_copy(
                src_ref=v_ref.at[from_x, from_y], dst_ref=one.at[to_x, to_y],
                send_sem=vsend.at[no], recv_sem=vrecv.at[no],
                device_id=target, device_id_type=MESH,
            ),
        )

    def arrivals(no, mx, my):
        other = moves.index((-mx, -my))
        at_x, at_y = hole(mx, size_x), hole(my, size_y)
        target = (gx + mx, gy + my, gv)
        return (
            pltpu.make_async_remote_copy(
                src_ref=auxe_ref.at[at_x, at_y], dst_ref=auxe_ref.at[at_x, at_y],
                send_sem=asend.at[other], recv_sem=arecv.at[other],
                device_id=target, device_id_type=MESH,
            ),
            pltpu.make_async_remote_copy(
                src_ref=one.at[at_x, at_y], dst_ref=one.at[at_x, at_y],
                send_sem=vsend.at[other], recv_sem=vrecv.at[other],
                device_id=target, device_id_type=MESH,
            ),
        )

    for no, (mx, my) in enumerate(moves):

        @pl.when(inside(mx, my))
        def _():
            for copy in copies(no, mx, my):
                copy.start()

        @pl.when(jnp.logical_not(inside(mx, my)))
        def _():
            at_x, at_y = hole(mx, size_x), hole(my, size_y)
            one[at_x, at_y] = jnp.zeros((at_x.size, at_y.size, vecs, depth), F32)
            auxe_ref[at_x, at_y] = jnp.zeros((at_x.size, at_y.size) + aux_ref.shape[2:], F32)

    auxe_ref[pl.ds(HALO, size_x), pl.ds(HALO, size_y)] = aux_ref[...]
    one[pl.ds(HALO, size_x), pl.ds(HALO, size_y)] = v_ref[...]

    for no, (mx, my) in enumerate(moves):

        @pl.when(inside(mx, my))
        def _():
            arrivals(no, mx, my)[0].wait_recv()

    def pick_k(ref, row, col):
        return ref[row, col, 0:1, :]

    def pick_u(ref, row, col):
        return ref[row, col]

    def gains(row, carry):
        around = smear_row(auxe_ref, row, 1, wide_y - 1, pick_k)
        for col in range(1, wide_y - 1):
            mid = pick_k(auxe_ref, row, col)
            below = around[col - 1] - (1.0 - SHIFT) * mid
            alive = mid > 0.0
            value = jnp.where(alive, OMEGA * mid / jnp.where(alive, below, 1.0), 0.0)
            gain[row, col] = jnp.broadcast_to(value, (vecs, depth))
        return carry

    lax.fori_loop(1, wide_x - 1, gains, 0)

    for no, (mx, my) in enumerate(moves):

        @pl.when(inside(mx, my))
        def _():
            arrivals(no, mx, my)[1].wait_recv()

    def scale(row, carry):
        for col in range(wide_y):
            one[row, col] = one[row, col] * jnp.broadcast_to(pick_k(auxe_ref, row, col), (vecs, depth))
        return carry

    lax.fori_loop(0, wide_x, scale, 0)

    def relaxed(ref, row, first, last):
        around = smear_row(ref, row, first, last, pick_u)
        result = []
        for col in range(first, last):
            factor = gain[row, col]
            result.append((1.0 - OMEGA - factor) * ref[row, col] + factor * around[col - first])
        return result

    source, target = one, two
    for sweep in range(1, SWEEPS):

        def step(row, carry, source=source, target=target, sweep=sweep):
            for no, value in enumerate(relaxed(source, row, sweep, wide_y - sweep)):
                target[row, sweep + no] = value
            return carry

        lax.fori_loop(sweep, wide_x - sweep, step, 0)
        source, target = target, source

    def field_copy(row, step):
        return pltpu.make_async_remote_copy(
            src_ref=out_ref.at[gv, row], dst_ref=out_ref.at[gv, row],
            send_sem=fsend.at[step - 1, row], recv_sem=frecv.at[step - 1, row],
            device_id=(gx, gy, lax.rem(gv + step, nv)), device_id_type=MESH,
        )

    rows = size_x + 2

    def last_sweep(row, carry):
        for no, value in enumerate(relaxed(source, row + SWEEPS, SWEEPS, wide_y - SWEEPS)):
            out_ref[gv, row, no] = value

        @pl.when(row >= 1)
        def _():
            for step in range(1, nv):
                field_copy(row - 1, step).start()

        return carry

    lax.fori_loop(0, rows, last_sweep, 0)
    for step in range(1, nv):
        field_copy(rows - 1, step).start()

    for no, (mx, my) in enumerate(moves):

        @pl.when(inside(mx, my))
        def _():
            for copy in copies(no, mx, my):
                copy.wait_send()

    for step in range(1, nv):
        origin = lax.rem(gv - step + nv, nv)
        for row in range(rows):
            field_copy(row, step).wait_send()
            pltpu.make_async_remote_copy(
                src_ref=out_ref.at[origin, row], dst_ref=out_ref.at[origin, row],
                send_sem=fsend.at[step - 1, row], recv_sem=frecv.at[step - 1, row],
                device_id=(gx, gy, origin), device_id_type=MESH,
            ).wait_recv()


def split(x):
    high = x.astype(BF16)
    return high, (x - high.astype(F32)).astype(BF16)


NT = (((1,), (1,)), ((), ()))
NN = (((1,), (0,)), ((), ()))


def dot(a, b, dims):
    return lax.dot_general(a, b, dims, preferred_element_type=F32)


def dot3(a, b, dims):
    return dot(a[0], b[0], dims) + dot(a[0], b[1], dims) + dot(a[1], b[0], dims)


def coarse_kernel(
    size_x, size_y, slots, f_ref, k_ref, c_ref, interp_ref, coarse_ref,
    hot, right_s, gram_s, lh, ll, rh, rl, ch, cl,
):
    nv, cols, vecs, depth = f_ref.shape
    wide_y = size_y + 2
    rows = GROUP * slots
    members = GROUP * nv * vecs
    count = gram_s.shape[0]
    band = size_y * slots

    def lanes(shape):
        return lax.broadcasted_iota(jnp.int32, shape, len(shape) - 1)

    def subs(shape):
        return lax.broadcasted_iota(jnp.int32, shape, len(shape) - 2)

    same = subs((rows, members)) // slots == lanes((rows, members)) // (nv * vecs)
    same_slots = subs((rows, rows)) // slots == lanes((rows, rows)) // slots
    own_lane = subs((rows, depth)) % slots == lanes((rows, depth))
    ones = jnp.ones((depth, depth), BF16)

    def start_of(no):
        return jnp.minimum(no * GROUP, cols - GROUP)

    def gather(no, carry):
        start = start_of(no)
        knots = k_ref[pl.ds(start, GROUP)]
        alive = knots > 0.0
        inverse = jnp.where(alive, 1.0 / jnp.where(alive, knots, 1.0), 0.0)
        field = jnp.concatenate(
            [f_ref[half, pl.ds(start, GROUP)] * inverse for half in range(nv)], axis=1
        ).reshape(members, depth)
        spots = jnp.broadcast_to(
            c_ref[pl.ds(start, GROUP)], (GROUP, slots, depth)
        ).reshape(rows, depth)
        spread = dot(jnp.where(own_lane, spots, 0.0).astype(BF16), ones, NN)
        onehot = jnp.where(spread == lanes((rows, depth)).astype(F32), 1.0, 0.0)
        hot[no] = onehot
        fh, fl = split(field)
        picked = onehot.astype(BF16)
        cvals = jnp.where(same, dot(picked, fh, NT) + dot(picked, fl, NT), 0.0)
        pair = split(cvals)
        right_s[no] = dot3(pair, (fh, fl), NN)
        gram = dot3(pair, pair, NT)
        gram_s[no] = jnp.sum(gram.reshape(GROUP, slots, rows), axis=0)
        return carry

    lax.fori_loop(0, count, gather, 0)

    shape = (count, slots, rows)
    lane = lanes(shape) % slots
    sub = subs(shape)
    system = gram_s[...]
    diagonal = jnp.sum(jnp.where(lane == sub, system, 0.0), axis=1)
    block = jnp.where(same_slots, 1.0, 0.0).astype(BF16)
    first = diagonal.astype(BF16)
    rest = diagonal - first.astype(F32)
    second = rest.astype(BF16)
    third = (rest - second.astype(F32)).astype(BF16)
    trace = dot(first, block, NN) + dot(second, block, NN) + dot(third, block, NN)
    ridge = RIDGE * trace / slots + 1e-06
    system = system + jnp.where(lane == sub, ridge[:, None, :], 0.0)
    flat = (count * slots, rows)
    base = lanes(flat) // slots * slots
    for pivot in range(slots):
        column = jnp.take_along_axis(
            system.reshape(flat), base + pivot, axis=1, mode="promise_in_bounds"
        ).reshape(shape)
        line = system[:, pivot : pivot + 1, :]
        here = lane[:, 0:1, :] == pivot
        line = jnp.where(here, 1.0, line) / column[:, pivot : pivot + 1, :]
        system = jnp.where(
            sub == pivot, line, jnp.where(lane == pivot, 0.0, system) - column * line
        )
    gram_s[...] = system

    def weigh(no, carry):
        start = start_of(no)
        inverse = jnp.where(
            same_slots,
            jnp.broadcast_to(gram_s[no][None], (GROUP, slots, rows)).reshape(rows, rows),
            0.0,
        )
        weights = dot3(split(inverse), split(right_s[no]), NN).reshape(GROUP, slots, depth)
        onehot = hot[no].reshape(GROUP, slots, depth)
        crow = jnp.sum(onehot, axis=1, keepdims=True)
        value = weights * (1.0 - crow) + onehot
        hot_cols = pl.ds(start, GROUP)
        ch[hot_cols] = value
        left = value * k_ref[hot_cols]
        high, low = split(left.reshape(rows, depth))
        lh[hot_cols] = high.reshape(GROUP, slots, depth)
        ll[hot_cols] = low.reshape(GROUP, slots, depth)
        high, low = split(smear_z(left.reshape(rows, depth)))
        rh[hot_cols] = high.reshape(GROUP, slots, depth)
        rl[hot_cols] = low.reshape(GROUP, slots, depth)
        return carry

    lax.fori_loop(0, count, weigh, 0)

    half = GROUP * slots
    groups = slots * slots // half
    sub_rows = slots // groups
    chosen = subs((sub_rows, half)) == lanes((sub_rows, half)) // slots

    def galerkin(row, carry):
        at = (row + 1) * wide_y
        mine = pl.ds(at + 1, size_y)
        own = ch[mine]
        interp_ref[row] = own
        across = k_ref[pl.ds(at, wide_y)] + ANISOTROPY[0] * (
            k_ref[pl.ds(at - wide_y, wide_y)] + k_ref[pl.ds(at + wide_y, wide_y)]
        )
        along = across[1 : size_y + 1] + ANISOTROPY[1] * (across[0:size_y] + across[2:])
        whole = smear_z(along.reshape(size_y, depth)).reshape(size_y, 1, depth)
        centre = own * (whole + SHIFT * k_ref[mine])
        left = (lh[mine].reshape(band, depth), ll[mine].reshape(band, depth))
        middle = dot3(left, split(centre.reshape(band, depth)), NT)
        for move_x in (-1, 0, 1):
            there = pl.ds(at + move_x * wide_y, wide_y)
            other = (
                rh[there].reshape(wide_y * slots, depth),
                rl[there].reshape(wide_y * slots, depth),
            )
            product = dot3(left, other, NT)
            for col in range(size_y):
                rows_here = slice(col * slots, (col + 1) * slots)
                for move_y in (-1, 0, 1):
                    weight = 1.0
                    if move_x != 0:
                        weight = weight * ANISOTROPY[0]
                    if move_y != 0:
                        weight = weight * ANISOTROPY[1]
                    begin = (col + 1 + move_y) * slots
                    tile = -weight * product[rows_here, begin : begin + slots]
                    if move_x == 0 and move_y == 0:
                        tile = tile + middle[rows_here, col * slots : (col + 1) * slots]
                    spread = jnp.concatenate([tile] * GROUP, axis=1)
                    parts = [
                        jnp.sum(
                            jnp.where(chosen, spread[g * sub_rows : (g + 1) * sub_rows], 0.0),
                            axis=0, keepdims=True,
                        )
                        for g in range(groups)
                    ]
                    order = 3 * (move_x + 1) + move_y + 1
                    coarse_ref[row, col, order : order + 1, :] = jnp.concatenate(parts, axis=1)
        return carry

    lax.fori_loop(0, size_x, galerkin, 0)


def body(nx, ny, nv, vectors, conductivity, c_points):
    vecs, size_x, size_y, depth = vectors.shape
    slots = c_points.shape[-1]
    turned = jnp.transpose(vectors, (1, 2, 0, 3))
    spots = jnp.pad(c_points.astype(F32), ((0, 0), (0, 0), (0, depth - slots)))
    aux = jnp.stack([conductivity, spots], axis=2)
    wide_x, wide_y = size_x + 2 * HALO, size_y + 2 * HALO
    vmem = pl.BlockSpec(memory_space=pltpu.VMEM)
    dma = pltpu.SemaphoreType.DMA
    field, auxe = pl.pallas_call(
        functools.partial(smooth_kernel, nx, ny, nv),
        out_shape=(
            jax.ShapeDtypeStruct((nv, size_x + 2, size_y + 2, vecs, depth), F32),
            jax.ShapeDtypeStruct((wide_x, wide_y, 2, depth), F32),
        ),
        in_specs=[vmem] * 2,
        out_specs=(vmem, vmem),
        scratch_shapes=[
            pltpu.VMEM((wide_x, wide_y, vecs, depth), F32),
            pltpu.VMEM((wide_x, wide_y, vecs, depth), F32),
            pltpu.VMEM((wide_x, wide_y, vecs, depth), F32),
            dma((8,)), dma((8,)), dma((8,)), dma((8,)),
            dma((nv, size_x + 2)), dma((nv, size_x + 2)),
        ],
        compiler_params=pltpu.CompilerParams(collective_id=0, has_side_effects=True),
        name="smooth",
    )(turned, aux)
    cols = (size_x + 2) * (size_y + 2)
    count = -(-cols // GROUP)
    rim = HALO - 1
    near = auxe[rim : wide_x - rim, rim : wide_y - rim].reshape(cols, 2, depth)
    rows = GROUP * slots
    return pl.pallas_call(
        functools.partial(coarse_kernel, size_x, size_y, slots),
        out_shape=(
            jax.ShapeDtypeStruct((size_x, size_y, slots, depth), F32),
            jax.ShapeDtypeStruct((size_x, size_y, 9, slots * slots), F32),
        ),
        in_specs=[vmem] * 3,
        out_specs=(vmem, vmem),
        scratch_shapes=[
            pltpu.VMEM((count, rows, depth), F32),
            pltpu.VMEM((count, rows, depth), F32),
            pltpu.VMEM((count, slots, rows), F32),
            pltpu.VMEM((cols, slots, depth), BF16),
            pltpu.VMEM((cols, slots, depth), BF16),
            pltpu.VMEM((cols, slots, depth), BF16),
            pltpu.VMEM((cols, slots, depth), BF16),
            pltpu.VMEM((cols, slots, depth), F32),
            pltpu.VMEM((8, 128), F32),
        ],
        name="coarse",
    )(field.reshape(nv, cols, vecs, depth), near[:, 0:1], near[:, 1:2])


def solution(mesh):
    placed = (P("vert", "gx", "gy", None), P("gx", "gy", None), P("gx", "gy", None))
    return jax.shard_map(
        functools.partial(body, mesh.shape["gx"], mesh.shape["gy"], mesh.shape["vert"]),
        mesh=mesh,
        in_specs=placed,
        out_specs=(P("gx", "gy", None, None), P("gx", "gy", None, None)),
        check_vma=False,
    )
```

time: 125 us -> 58.9 us (0.47)
  Pallas kernels: 0 us -> 50.8 us
  starting transfers between devices: 48.5 us -> 0 us
  waiting for transfers between devices: 25.8 us -> 0 us
  matrix products: 16.8 us -> 0 us
  other arithmetic: 15.8 us -> 2.26 us
  blocking collectives: 8.71 us -> 0 us
  local copies, waits for them, and re-layouts: 7.09 us -> 4.88 us
    pallas_call x0 -> x2, Pallas kernels: none -> 50.8 us  [the longest x1 26 us: body(): pl.pallas_call(functools.partial(smooth_kernel, nx, ny, nv), out_shape=(j...]
    ppermute x20 -> x0, starting transfers between devices: 48.5 us -> none  [the longest x10 32.2 us: padded_2(): lax.ppermute(lax.slice_in_dim(block, block.shape[dim] - width, None, axis...]
    ppermute x20 -> x0, waiting for transfers between devices: 25.8 us -> none  [the longest x10 25.8 us: padded_2(): lax.ppermute(lax.slice_in_dim(block, 0, width, axis=dim), axis, backward)]
    dot_general x12 -> x0, matrix products: 16.8 us -> none  [the longest x9 14.5 us: galerkin(): jnp.einsum('xyiz,xyjz->xyij', interp, image, precision=lax.Precision.HIGH...]
    all_gather x1 -> x0, blocking collectives: 8.71 us -> none  [body(): whole = lax.all_gather(field, 'vert', axis=0, tiled=True)]
    unnamed x5 -> x0, other arithmetic: 4.28 us -> none
    div x25 -> x0, other arithmetic: 3.75 us -> none  [the longest x1 2.44 us: batched_solve(): backward[row] = total / lower[row][row][:, None]]
    another operation x11 -> x0, local copies, waits for them, and re-layouts: 3.35 us -> none  [the longest x10 3.34 us: galerkin(): return jnp.stack(blocks, axis=2)]
  transfers between devices with their start and end apart: 20 -> 0, of which waited for: 8 -> 0; matrix products, arithmetic and copies ran while one was open for 2% -> 0% of each run, Pallas kernels for 0% -> 0%
where the time goes in v1:
time: 58.9 us; the launch traced here: 58.6 us
  Pallas kernels  50.8 us (86%)
  local copies, waits for them, and re-layouts  4.88 us (8%)
  other arithmetic  2.26 us (4%)
  between operations  0.65 us (1%)
    pallas_call x1, Pallas kernels, body(): pl.pallas_call(functools.partial(smooth_kernel, nx, ny, nv), out_shape=(j...  26 us
    pallas_call x1, Pallas kernels, body(): pl.pallas_call(functools.partial(coarse_kernel, size_x, size_y, slots), o...  24.8 us
    pallas_call x1, local copies, waits for them, and re-layouts, body(): pl.pallas_call(functools.partial(coarse_kernel, size_x, size_y, slots), o...  2.39 us
    another operation x1, other arithmetic, body(): aux = jnp.stack([conductivity, spots], axis=2)  1.45 us

profile of v1, /device:TPU:1, one launch (start us, length us, event | category | flops | bytes accessed | tf_op | source)
XLA Modules:
  0.0 58.6 jit_solution(16456801163276468749)
XLA Ops:
  0.6 0.0 copy-start
  0.6 0.8 %convert_element_type.5 = f32[8,8,16]{2,1,0:T(8,128)S(1)} convert(s32[8,8,16]{2,1,0:T(8,128)} %param.5) | non-fusion elementwise | flops 1024 | bytes 8192 | tf_op jit(solution)/shard_map/convert_element_type | solution.py:411
  1.5 1.5 %pad_maximum_fusion.aux_ref = f32[8,8,2,128]{3,2,1,0:T(2,128)} fusion(f32[8,8,1,128]{3,2,1,0:T(1,128)S(1)} %bitcast.10, f32[8,8,1,128]{3,2,1,0:T(1,128)} %bitcast.11), kind=kLoop, calls=%fused_computation.1 | loop fusion | flops 16384 | bytes 131072 | tf_op jit(solution)/shard_map/stack | solution.py:412
  2.9 0.0 copy-done
  2.9 0.9 %copy.8 = f32[8,8,8,128]{3,0,2,1:T(8,128)} copy(f32[8,8,8,128]{3,2,1,0:T(8,128)S(1)} %copy-done) | data formatting | bytes 524288 | tf_op args[0]
  3.8 26.0 %smooth.1 = (f32[2,10,10,8,128]{4,3,2,1,0:T(8,128)}, f32[16,16,2,128]{3,2,1,0:T(2,128)}) custom-call(f32[8,8,8,128]{3,2,1,0:T(8,128)} %bitcast.7, f32[8,8,2,128]{3,2,1,0:T(2,128)} %pad_maximum_fusion.aux_ref), custom_call_target="tpu_custom_call" | custom-call | tf_op jit(solution)/shard_map/smooth/pallas_call | solution.py:416
  29.8 0.9 %slice.9 = f32[10,10,2,128]{3,2,1,0:T(2,128)S(1)} slice(f32[16,16,2,128]{3,2,1,0:T(2,128)} %get-tuple-element.5), slice={[3:13], [3:13], [0:2], [0:128]} | slice | bytes 204800 | tf_op jit(solution)/shard_map/slice | solution.py:437
  30.7 0.7 %fusion = (f32[100,1,128]{2,1,0:T(1,128)}, f32[100,1,128]{2,1,0:T(1,128)}) fusion(f32[100,2,128]{2,1,0:T(2,128)S(1)} %bitcast.9), kind=kLoop, calls=%fused_computation.2 | loop fusion | bytes 204800 | tf_op jit(solution)/shard_map/slice | solution.py:459
  31.4 24.8 %coarse.1 = (f32[8,8,16,128]{3,2,1,0:T(8,128)}, f32[8,8,9,256]{3,2,1,0:T(8,128)}) custom-call(f32[2,100,8,128]{3,2,1,0:T(8,128)} %bitcast.8, f32[100,1,128]{2,1,0:T(1,128)} %get-tuple-element.9.k_ref, f32[100,1,128]{2,1,0:T(1,128)} %get-tuple-element.8.c_ref), custom_call_target="tpu_custom_call" | custom-call | tf_op jit(solution)/shard_map/coarse/pallas_call | solution.py:439
  56.2 2.4 %copy.6 = f32[8,8,9,256]{3,1,2,0:T(8,128)} copy(f32[8,8,9,256]{3,2,1,0:T(8,128)} %get-tuple-element.7) | data formatting | bytes 1179648 | tf_op jit(solution)/shard_map/coarse/pallas_call | solution.py:439
  (1 shorter events, 0.0 us)
Async XLA Ops:
  0.6 2.3 %copy-start = (f32[8,8,8,128]{3,2,1,0:T(8,128)S(1)}, f32[8,8,8,128]{3,2,1,0:T(8,128)}, u32[]{:S(2)}) copy-start(f32[8,8,8,128]{3,2,1,0:T(8,128)} %param.3) | copy-start | bytes 786436

commit v2 on v1

--- a/solution.py
+++ b/solution.py
@@ -14,6 +14,7 @@
 RIDGE = 0.1
 HALO = SWEEPS + 1
 GROUP = 8
+UNROLL = True
 MESH = pl.DeviceIdType.MESH
 F32 = jnp.float32
 BF16 = jnp.bfloat16
@@ -55,8 +56,8 @@
 
 
 def smooth_kernel(
-    nx, ny, nv, v_ref, aux_ref, out_ref, auxe_ref,
-    one, two, gain, vsend, vrecv, asend, arecv, fsend, frecv,
+    nx, ny, nv, v_ref, k_ref, c_ref, out_ref, knots_ref, spots_ref,
+    one, two, gain, wide_k, wide_c, ksend, krecv, csend, crecv, vsend, vrecv, fsend, frecv,
 ):
     size_x, size_y, vecs, depth = v_ref.shape
     wide_x, wide_y = size_x + 2 * HALO, size_y + 2 * HALO
@@ -86,61 +87,54 @@
         )
     pl.semaphore_wait(barrier, total)
 
-    def copies(no, mx, my):
+    kinds = (
+        (k_ref, wide_k, ksend, krecv), (v_ref, one, vsend, vrecv), (c_ref, wide_c, csend, crecv),
+    )
+
+    def departure(kind, no):
+        mx, my = moves[no]
+        source, target, send, recv = kinds[kind]
         from_x, to_x = span(mx, size_x)
         from_y, to_y = span(my, size_y)
-        target = (gx + mx, gy + my, gv)
-        return (
-            pltpu.make_async_remote_copy(
-                src_ref=aux_ref.at[from_x, from_y], dst_ref=auxe_ref.at[to_x, to_y],
-                send_sem=asend.at[no], recv_sem=arecv.at[no],
-                device_id=target, device_id_type=MESH,
-            ),
-            pltpu.make_async_remote_copy(
-                src_ref=v_ref.at[from_x, from_y], dst_ref=one.at[to_x, to_y],
-                send_sem=vsend.at[no], recv_sem=vrecv.at[no],
-                device_id=target, device_id_type=MESH,
-            ),
-        )
-
-    def arrivals(no, mx, my):
+        return pltpu.make_async_remote_copy(
+            src_ref=source.at[from_x, from_y], dst_ref=target.at[to_x, to_y],
+            send_sem=send.at[no], recv_sem=recv.at[no],
+            device_id=(gx + mx, gy + my, gv), device_id_type=MESH,
+        )
+
+    def arrival(kind, no):
+        mx, my = moves[no]
         other = moves.index((-mx, -my))
-        at_x, at_y = hole(mx, size_x), hole(my, size_y)
-        target = (gx + mx, gy + my, gv)
-        return (
-            pltpu.make_async_remote_copy(
-                src_ref=auxe_ref.at[at_x, at_y], dst_ref=auxe_ref.at[at_x, at_y],
-                send_sem=asend.at[other], recv_sem=arecv.at[other],
-                device_id=target, device_id_type=MESH,
-            ),
-            pltpu.make_async_remote_copy(
-                src_ref=one.at[at_x, at_y], dst_ref=one.at[at_x, at_y],
-                send_sem=vsend.at[other], recv_sem=vrecv.at[other],
-                device_id=target, device_id_type=MESH,
-            ),
+        _, target, send, recv = kinds[kind]
+        place = target.at[hole(mx, size_x), hole(my, size_y)]
+        return pltpu.make_async_remote_copy(
+            src_ref=place, dst_ref=place, send_sem=send.at[other], recv_sem=recv.at[other],
+            device_id=(gx + mx, gy + my, gv), device_id_type=MESH,
         )
 
     for no, (mx, my) in enumerate(moves):
 
         @pl.when(inside(mx, my))
         def _():
-            for copy in copies(no, mx, my):
-                copy.start()
+            for kind in range(3):
+                departure(kind, no).start()
 
         @pl.when(jnp.logical_not(inside(mx, my)))
         def _():
             at_x, at_y = hole(mx, size_x), hole(my, size_y)
-            one[at_x, at_y] = jnp.zeros((at_x.size, at_y.size, vecs, depth), F32)
-            auxe_ref[at_x, at_y] = jnp.zeros((at_x.size, at_y.size) + aux_ref.shape[2:], F32)
-
-    auxe_ref[pl.ds(HALO, size_x), pl.ds(HALO, size_y)] = aux_ref[...]
-    one[pl.ds(HALO, size_x), pl.ds(HALO, size_y)] = v_ref[...]
+            for source, target, _, _ in kinds:
+                target[at_x, at_y] = jnp.zeros(
+                    (at_x.size, at_y.size) + source.shape[2:], source.dtype
+                )
+
+    for source, target, _, _ in kinds:
+        target[pl.ds(HALO, size_x), pl.ds(HALO, size_y)] = source[...]
 
     for no, (mx, my) in enumerate(moves):
 
         @pl.when(inside(mx, my))
         def _():
-            arrivals(no, mx, my)[0].wait_recv()
+            arrival(0, no).wait_recv()
 
     def pick_k(ref, row, col):
         return ref[row, col, 0:1, :]
@@ -149,9 +143,9 @@
         return ref[row, col]
 
     def gains(row, carry):
-        around = smear_row(auxe_ref, row, 1, wide_y - 1, pick_k)
+        around = smear_row(wide_k, row, 1, wide_y - 1, pick_k)
         for col in range(1, wide_y - 1):
-            mid = pick_k(auxe_ref, row, col)
+            mid = pick_k(wide_k, row, col)
             below = around[col - 1] - (1.0 - SHIFT) * mid
             alive = mid > 0.0
             value = jnp.where(alive, OMEGA * mid / jnp.where(alive, below, 1.0), 0.0)
@@ -164,11 +158,12 @@
 
         @pl.when(inside(mx, my))
         def _():
-            arrivals(no, mx, my)[1].wait_recv()
+            arrival(1, no).wait_recv()
+            arrival(2, no).wait_recv()
 
     def scale(row, carry):
         for col in range(wide_y):
-            one[row, col] = one[row, col] * jnp.broadcast_to(pick_k(auxe_ref, row, col), (vecs, depth))
+            one[row, col] = one[row, col] * jnp.broadcast_to(pick_k(wide_k, row, col), (vecs, depth))
         return carry
 
     lax.fori_loop(0, wide_x, scale, 0)
@@ -216,12 +211,16 @@
     for step in range(1, nv):
         field_copy(rows - 1, step).start()
 
+    rim_x, rim_y = pl.ds(HALO - 1, size_x + 2), pl.ds(HALO - 1, size_y + 2)
+    knots_ref[...] = wide_k[rim_x, rim_y]
+    spots_ref[...] = wide_c[rim_x, rim_y]
+
     for no, (mx, my) in enumerate(moves):
 
         @pl.when(inside(mx, my))
         def _():
-            for copy in copies(no, mx, my):
-                copy.wait_send()
+            for kind in range(3):
+                departure(kind, no).wait_send()
 
     for step in range(1, nv):
         origin = lax.rem(gv - step + nv, nv)
@@ -253,13 +252,14 @@
 
 def coarse_kernel(
     size_x, size_y, slots, f_ref, k_ref, c_ref, interp_ref, coarse_ref,
-    hot, right_s, gram_s, lh, ll, rh, rl, ch, cl,
+    hot, right_s, gram_s, lh, ll, rh, rl, ch,
 ):
     nv, cols, vecs, depth = f_ref.shape
     wide_y = size_y + 2
     rows = GROUP * slots
     members = GROUP * nv * vecs
     count = gram_s.shape[0]
+    padded = -(-wide_y // GROUP) * GROUP
     band = size_y * slots
 
     def lanes(shape):
@@ -270,8 +270,8 @@
 
     same = subs((rows, members)) // slots == lanes((rows, members)) // (nv * vecs)
     same_slots = subs((rows, rows)) // slots == lanes((rows, rows)) // slots
-    own_lane = subs((rows, depth)) % slots == lanes((rows, depth))
-    ones = jnp.ones((depth, depth), BF16)
+    own_lane = subs((rows, slots)) % slots == lanes((rows, slots))
+    ones = jnp.ones((slots, depth), BF16)
 
     def start_of(no):
         return jnp.minimum(no * GROUP, cols - GROUP)
@@ -285,8 +285,8 @@
             [f_ref[half, pl.ds(start, GROUP)] * inverse for half in range(nv)], axis=1
         ).reshape(members, depth)
         spots = jnp.broadcast_to(
-            c_ref[pl.ds(start, GROUP)], (GROUP, slots, depth)
-        ).reshape(rows, depth)
+            c_ref[pl.ds(start, GROUP)].astype(F32), (GROUP, slots, slots)
+        ).reshape(rows, slots)
         spread = dot(jnp.where(own_lane, spots, 0.0).astype(BF16), ones, NN)
         onehot = jnp.where(spread == lanes((rows, depth)).astype(F32), 1.0, 0.0)
         hot[no] = onehot
@@ -299,7 +299,7 @@
         gram_s[no] = jnp.sum(gram.reshape(GROUP, slots, rows), axis=0)
         return carry
 
-    lax.fori_loop(0, count, gather, 0)
+    lax.fori_loop(0, count, gather, 0, unroll=UNROLL)
 
     shape = (count, slots, rows)
     lane = lanes(shape) % slots
@@ -350,12 +350,33 @@
         rl[hot_cols] = low.reshape(GROUP, slots, depth)
         return carry
 
-    lax.fori_loop(0, count, weigh, 0)
+    lax.fori_loop(0, count, weigh, 0, unroll=UNROLL)
 
     half = GROUP * slots
     groups = slots * slots // half
-    sub_rows = slots // groups
-    chosen = subs((sub_rows, half)) == lanes((sub_rows, half)) // slots
+    tall = (GROUP, half)
+    pick_row = lanes(tall) // slots
+    out_row = subs(tall)
+
+    def merge(tiles):
+        hop = GROUP // 2
+        while hop >= 1:
+            up = out_row // hop % 2 == 1
+            straight = up == (pick_row // hop % 2 == 1)
+            merged = []
+            for no in range(hop):
+                one, two = tiles[no], tiles[no + hop]
+                same_place = jnp.where(up, two, one)
+                moved = jnp.where(up, one, two)
+                down = pltpu.roll(moved, hop, 0)
+                if 2 * hop != GROUP:
+                    down = jnp.where(up, down, pltpu.roll(moved, GROUP - hop, 0))
+                merged.append(jnp.where(straight, same_place, down))
+            tiles = merged
+            hop //= 2
+        return tiles[0]
+
+    block_lane = lanes((slots, half)) % slots
 
     def galerkin(row, carry):
         at = (row + 1) * wide_y
@@ -367,38 +388,47 @@
         )
         along = across[1 : size_y + 1] + ANISOTROPY[1] * (across[0:size_y] + across[2:])
         whole = smear_z(along.reshape(size_y, depth)).reshape(size_y, 1, depth)
-        centre = own * (whole + SHIFT * k_ref[mine])
         left = (lh[mine].reshape(band, depth), ll[mine].reshape(band, depth))
+        right = rh[mine].astype(F32) + rl[mine].astype(F32)
+        centre = right - own * (whole + SHIFT * k_ref[mine])
         middle = dot3(left, split(centre.reshape(band, depth)), NT)
         for move_x in (-1, 0, 1):
-            there = pl.ds(at + move_x * wide_y, wide_y)
+            there = pl.ds(at + move_x * wide_y, padded)
             other = (
-                rh[there].reshape(wide_y * slots, depth),
-                rl[there].reshape(wide_y * slots, depth),
+                rh[there].reshape(padded * slots, depth),
+                rl[there].reshape(padded * slots, depth),
             )
             product = dot3(left, other, NT)
-            for col in range(size_y):
-                rows_here = slice(col * slots, (col + 1) * slots)
-                for move_y in (-1, 0, 1):
-                    weight = 1.0
-                    if move_x != 0:
-                        weight = weight * ANISOTROPY[0]
-                    if move_y != 0:
-                        weight = weight * ANISOTROPY[1]
-                    begin = (col + 1 + move_y) * slots
-                    tile = -weight * product[rows_here, begin : begin + slots]
-                    if move_x == 0 and move_y == 0:
-                        tile = tile + middle[rows_here, col * slots : (col + 1) * slots]
-                    spread = jnp.concatenate([tile] * GROUP, axis=1)
+            for move_y in (-1, 0, 1):
+                weight = 1.0
+                if move_x != 0:
+                    weight = weight * ANISOTROPY[0]
+                if move_y != 0:
+                    weight = weight * ANISOTROPY[1]
+                order = 3 * (move_x + 1) + move_y + 1
+                for chunk in range(0, size_y, GROUP):
+                    spread = []
+                    for col in range(chunk, chunk + GROUP):
+                        central = move_x == 0 and move_y == 0
+                        origin = middle if central else product
+                        place = col if central else col + 1 + move_y
+                        first_lane = place // GROUP * half
+                        values = origin[
+                            col * slots : (col + 1) * slots, first_lane : first_lane + half
+                        ]
+                        spread.append(
+                            jnp.take_along_axis(
+                                values, block_lane + place % GROUP * slots, axis=1,
+                                mode="promise_in_bounds",
+                            )
+                        )
                     parts = [
-                        jnp.sum(
-                            jnp.where(chosen, spread[g * sub_rows : (g + 1) * sub_rows], 0.0),
-                            axis=0, keepdims=True,
-                        )
+                        merge([tile[g * GROUP : (g + 1) * GROUP] for tile in spread])
                         for g in range(groups)
                     ]
-                    order = 3 * (move_x + 1) + move_y + 1
-                    coarse_ref[row, col, order : order + 1, :] = jnp.concatenate(parts, axis=1)
+                    coarse_ref[row, order, chunk : chunk + GROUP, :] = -weight * jnp.concatenate(
+                        parts, axis=1
+                    )
         return carry
 
     lax.fori_loop(0, size_x, galerkin, 0)
@@ -408,39 +438,39 @@
     vecs, size_x, size_y, depth = vectors.shape
     slots = c_points.shape[-1]
     turned = jnp.transpose(vectors, (1, 2, 0, 3))
-    spots = jnp.pad(c_points.astype(F32), ((0, 0), (0, 0), (0, depth - slots)))
-    aux = jnp.stack([conductivity, spots], axis=2)
     wide_x, wide_y = size_x + 2 * HALO, size_y + 2 * HALO
+    cols = (size_x + 2) * (size_y + 2)
     vmem = pl.BlockSpec(memory_space=pltpu.VMEM)
     dma = pltpu.SemaphoreType.DMA
-    field, auxe = pl.pallas_call(
+    field, knots, spots = pl.pallas_call(
         functools.partial(smooth_kernel, nx, ny, nv),
         out_shape=(
             jax.ShapeDtypeStruct((nv, size_x + 2, size_y + 2, vecs, depth), F32),
-            jax.ShapeDtypeStruct((wide_x, wide_y, 2, depth), F32),
+            jax.ShapeDtypeStruct((size_x + 2, size_y + 2, 1, depth), F32),
+            jax.ShapeDtypeStruct((size_x + 2, size_y + 2, 1, slots), jnp.int32),
         ),
-        in_specs=[vmem] * 2,
-        out_specs=(vmem, vmem),
+        in_specs=[vmem] * 3,
+        out_specs=(vmem,) * 3,
         scratch_shapes=[
             pltpu.VMEM((wide_x, wide_y, vecs, depth), F32),
             pltpu.VMEM((wide_x, wide_y, vecs, depth), F32),
             pltpu.VMEM((wide_x, wide_y, vecs, depth), F32),
-            dma((8,)), dma((8,)), dma((8,)), dma((8,)),
+            pltpu.VMEM((wide_x, wide_y, 1, depth), F32),
+            pltpu.VMEM((wide_x, wide_y, 1, slots), jnp.int32),
+            dma((8,)), dma((8,)), dma((8,)), dma((8,)), dma((8,)), dma((8,)),
             dma((nv, size_x + 2)), dma((nv, size_x + 2)),
         ],
         compiler_params=pltpu.CompilerParams(collective_id=0, has_side_effects=True),
         name="smooth",
-    )(turned, aux)
-    cols = (size_x + 2) * (size_y + 2)
+    )(turned, conductivity[:, :, None, :], c_points[:, :, None, :])
     count = -(-cols // GROUP)
-    rim = HALO - 1
-    near = auxe[rim : wide_x - rim, rim : wide_y - rim].reshape(cols, 2, depth)
     rows = GROUP * slots
-    return pl.pallas_call(
+    more = cols + 2 * GROUP
+    interp, coarse = pl.pallas_call(
         functools.partial(coarse_kernel, size_x, size_y, slots),
         out_shape=(
             jax.ShapeDtypeStruct((size_x, size_y, slots, depth), F32),
-            jax.ShapeDtypeStruct((size_x, size_y, 9, slots * slots), F32),
+            jax.ShapeDtypeStruct((size_x, 9, size_y, slots * slots), F32),
         ),
         in_specs=[vmem] * 3,
         out_specs=(vmem, vmem),
@@ -448,15 +478,19 @@
             pltpu.VMEM((count, rows, depth), F32),
             pltpu.VMEM((count, rows, depth), F32),
             pltpu.VMEM((count, slots, rows), F32),
-            pltpu.VMEM((cols, slots, depth), BF16),
-            pltpu.VMEM((cols, slots, depth), BF16),
-            pltpu.VMEM((cols, slots, depth), BF16),
-            pltpu.VMEM((cols, slots, depth), BF16),
-            pltpu.VMEM((cols, slots, depth), F32),
-            pltpu.VMEM((8, 128), F32),
+            pltpu.VMEM((more, slots, depth), BF16),
+            pltpu.VMEM((more, slots, depth), BF16),
+            pltpu.VMEM((more, slots, depth), BF16),
+            pltpu.VMEM((more, slots, depth), BF16),
+            pltpu.VMEM((more, slots, depth), F32),
         ],
         name="coarse",
-    )(field.reshape(nv, cols, vecs, depth), near[:, 0:1], near[:, 1:2])
+    )(
+        field.reshape(nv, cols, vecs, depth),
+        knots.reshape(cols, 1, depth),
+        spots.reshape(cols, 1, slots),
+    )
+    return interp, jnp.transpose(coarse, (0, 2, 1, 3))
 
 
 def solution(mesh):

time: 58.9 us -> 42.8 us (0.73)
  Pallas kernels: 50.8 us -> 40.2 us
  local copies, waits for them, and re-layouts: 4.88 us -> 1.81 us
  other arithmetic: 2.26 us -> 0 us
    pallas_call x1, Pallas kernels: 24.8 us -> 14 us  [body(): pl.pallas_call(functools.partial(coarse_kernel, size_x, size_y, slots), o...]
    pallas_call x1 -> x0, local copies, waits for them, and re-layouts: 2.39 us -> none  [body(): pl.pallas_call(functools.partial(coarse_kernel, size_x, size_y, slots), o...]
    slice x2 -> x0, local copies, waits for them, and re-layouts: 1.63 us -> none  [the longest x1 0.91 us: body(): near = auxe[rim:wide_x - rim, rim:wide_y - rim].reshape(cols, 2, depth)]
    another operation x1 -> x0, other arithmetic: 1.45 us -> none  [body(): aux = jnp.stack([conductivity, spots], axis=2)]
    unnamed x3 -> x1, local copies, waits for them, and re-layouts: 0.86 us -> 1.81 us
    convert_element_type x1 -> x0, other arithmetic: 0.8 us -> none  [body(): spots = jnp.pad(c_points.astype(F32), ((0, 0), (0, 0), (0, depth - slots)))]
where the time goes in v2:
time: 42.8 us; the launch traced here: 42.6 us
  Pallas kernels  40.2 us (94%)
  local copies, waits for them, and re-layouts  1.81 us (4%)
  between operations  0.64 us (1%)
    pallas_call x1, Pallas kernels, body(): pl.pallas_call(functools.partial(smooth_kernel, nx, ny, nv), out_shape=(j...  26.2 us
    pallas_call x1, Pallas kernels, body(): pl.pallas_call(functools.partial(coarse_kernel, size_x, size_y, slots), o...  14 us
    unnamed x1, local copies, waits for them, and re-layouts  1.81 us

profile of v2, /device:TPU:1, one launch (start us, length us, event | category | flops | bytes accessed | tf_op | source)
XLA Modules:
  0.0 42.6 jit_solution(6936177380897499820)
XLA Ops:
  0.6 1.8 %copy.7 = f32[8,8,8,128]{3,0,2,1:T(8,128)} copy(f32[8,8,8,128]{3,2,1,0:T(8,128)} %param.3) | data formatting | bytes 524288 | tf_op args[0]
  2.4 26.2 %smooth.1 = (f32[2,10,10,8,128]{4,3,2,1,0:T(8,128)}, f32[10,10,1,128]{3,2,1,0:T(1,128)}, s32[10,10,1,16]{3,2,1,0:T(1,128)}) custom-call(f32[8,8,8,128]{3,2,1,0:T(8,128)} %bitcast.9, f32[8,8,1,128]{3,2,1,0:T(1,128)} %bitcast.13, s32[8,8,1,16]{3,2,1,0:T(1,128)} %bitcast.14), custom_call_target="tpu_custom_call" | custom-call | tf_op jit(solution)/shard_map/smooth/pallas_call | solution.py:445
  28.6 14.0 %coarse.1 = (f32[8,8,16,128]{3,2,1,0:T(8,128)}, f32[8,9,8,256]{3,2,1,0:T(8,128)}) custom-call(f32[2,100,8,128]{3,2,1,0:T(8,128)} %bitcast.10, f32[100,1,128]{2,1,0:T(1,128)} %bitcast.11, s32[100,1,16]{2,1,0:T(1,128)} %bitcast.12), custom_call_target="tpu_custom_call" | custom-call | tf_op jit(solution)/shard_map/coarse/pallas_call | solution.py:469

commit v3 on v2

--- a/solution.py
+++ b/solution.py
@@ -12,7 +12,7 @@
 OMEGA = 0.6
 SHIFT = 0.5
 RIDGE = 0.1
-HALO = SWEEPS + 1
+HALO = SWEEPS
 GROUP = 8
 UNROLL = True
 MESH = pl.DeviceIdType.MESH
@@ -55,9 +55,16 @@
     return pl.ds(size + HALO, HALO) if move > 0 else pl.ds(0, HALO)
 
 
+def rim(move, size):
+    if move == 0:
+        return pl.ds(1, size)
+    return pl.ds(size + 1, 1) if move > 0 else pl.ds(0, 1)
+
+
 def smooth_kernel(
     nx, ny, nv, v_ref, k_ref, c_ref, out_ref, knots_ref, spots_ref,
-    one, two, gain, wide_k, wide_c, ksend, krecv, csend, crecv, vsend, vrecv, fsend, frecv,
+    one, two, gain, wide_k, wide_c, ksend, krecv, csend, crecv, vsend, vrecv,
+    fsend, frecv, hsend, hrecv,
 ):
     size_x, size_y, vecs, depth = v_ref.shape
     wide_x, wide_y = size_x + 2 * HALO, size_y + 2 * HALO
@@ -126,6 +133,8 @@
                 target[at_x, at_y] = jnp.zeros(
                     (at_x.size, at_y.size) + source.shape[2:], source.dtype
                 )
+            rim_x, rim_y = rim(mx, size_x), rim(my, size_y)
+            out_ref[:, rim_x, rim_y] = jnp.zeros((nv, rim_x.size, rim_y.size, vecs, depth), F32)
 
     for source, target, _, _ in kinds:
         target[pl.ds(HALO, size_x), pl.ds(HALO, size_y)] = source[...]
@@ -187,50 +196,88 @@
         lax.fori_loop(sweep, wide_x - sweep, step, 0)
         source, target = target, source
 
-    def field_copy(row, step):
+    def last_sweep(row, carry):
+        for no, value in enumerate(relaxed(source, row, SWEEPS, wide_y - SWEEPS)):
+            out_ref[gv, row - SWEEPS + 1, no + 1] = value
+        return carry
+
+    lax.fori_loop(SWEEPS, wide_x - SWEEPS, last_sweep, 0)
+
+    pieces = (
+        (pl.ds(1, 1), pl.ds(1, size_y)),
+        (pl.ds(size_x, 1), pl.ds(1, size_y)),
+        (pl.ds(2, size_x - 2), pl.ds(1, 1)),
+        (pl.ds(2, size_x - 2), pl.ds(size_y, 1)),
+        (pl.ds(2, size_x - 2), pl.ds(2, size_y - 2)),
+    )
+
+    def piece_copy(no, step, half):
+        place = out_ref.at[(half,) + pieces[no]]
         return pltpu.make_async_remote_copy(
-            src_ref=out_ref.at[gv, row], dst_ref=out_ref.at[gv, row],
-            send_sem=fsend.at[step - 1, row], recv_sem=frecv.at[step - 1, row],
+            src_ref=place, dst_ref=place,
+            send_sem=fsend.at[step - 1, no], recv_sem=frecv.at[step - 1, no],
             device_id=(gx, gy, lax.rem(gv + step, nv)), device_id_type=MESH,
         )
 
-    rows = size_x + 2
-
-    def last_sweep(row, carry):
-        for no, value in enumerate(relaxed(source, row + SWEEPS, SWEEPS, wide_y - SWEEPS)):
-            out_ref[gv, row, no] = value
-
-        @pl.when(row >= 1)
-        def _():
-            for step in range(1, nv):
-                field_copy(row - 1, step).start()
-
-        return carry
-
-    lax.fori_loop(0, rows, last_sweep, 0)
-    for step in range(1, nv):
-        field_copy(rows - 1, step).start()
+    def edge(move, size):
+        if move == 0:
+            return pl.ds(1, size), pl.ds(1, size)
+        if move > 0:
+            return pl.ds(size, 1), pl.ds(0, 1)
+        return pl.ds(1, 1), pl.ds(size + 1, 1)
+
+    def rim_departure(step, half, no):
+        mx, my = moves[no]
+        from_x, to_x = edge(mx, size_x)
+        from_y, to_y = edge(my, size_y)
+        return pltpu.make_async_remote_copy(
+            src_ref=out_ref.at[half, from_x, from_y], dst_ref=out_ref.at[half, to_x, to_y],
+            send_sem=hsend.at[step, no], recv_sem=hrecv.at[step, no],
+            device_id=(gx + mx, gy + my, gv), device_id_type=MESH,
+        )
+
+    def rim_arrival(step, half, no):
+        mx, my = moves[no]
+        other = moves.index((-mx, -my))
+        place = out_ref.at[half, edge(-mx, size_x)[1], edge(-my, size_y)[1]]
+        return pltpu.make_async_remote_copy(
+            src_ref=place, dst_ref=place,
+            send_sem=hsend.at[step, other], recv_sem=hrecv.at[step, other],
+            device_id=(gx + mx, gy + my, gv), device_id_type=MESH,
+        )
+
+    for no in range(len(pieces)):
+        for step in range(1, nv):
+            piece_copy(no, step, gv).start()
+    for step in range(nv):
+        half = lax.rem(gv - step + nv, nv)
+        if step > 0:
+            for no in range(len(pieces) - 1):
+                piece_copy(no, step, half).wait_recv()
+        for no, (mx, my) in enumerate(moves):
+
+            @pl.when(inside(mx, my))
+            def _():
+                rim_departure(step, half, no).start()
 
     rim_x, rim_y = pl.ds(HALO - 1, size_x + 2), pl.ds(HALO - 1, size_y + 2)
     knots_ref[...] = wide_k[rim_x, rim_y]
     spots_ref[...] = wide_c[rim_x, rim_y]
 
+    for step in range(1, nv):
+        piece_copy(len(pieces) - 1, step, lax.rem(gv - step + nv, nv)).wait_recv()
+        for no in range(len(pieces)):
+            piece_copy(no, step, gv).wait_send()
     for no, (mx, my) in enumerate(moves):
 
         @pl.when(inside(mx, my))
         def _():
             for kind in range(3):
                 departure(kind, no).wait_send()
-
-    for step in range(1, nv):
-        origin = lax.rem(gv - step + nv, nv)
-        for row in range(rows):
-            field_copy(row, step).wait_send()
-            pltpu.make_async_remote_copy(
-                src_ref=out_ref.at[origin, row], dst_ref=out_ref.at[origin, row],
-                send_sem=fsend.at[step - 1, row], recv_sem=frecv.at[step - 1, row],
-                device_id=(gx, gy, origin), device_id_type=MESH,
-            ).wait_recv()
+            for step in range(nv):
+                half = lax.rem(gv - step + nv, nv)
+                rim_arrival(step, half, no).wait_recv()
+                rim_departure(step, half, no).wait_send()
 
 
 def split(x):
@@ -458,7 +505,7 @@
             pltpu.VMEM((wide_x, wide_y, 1, depth), F32),
             pltpu.VMEM((wide_x, wide_y, 1, slots), jnp.int32),
             dma((8,)), dma((8,)), dma((8,)), dma((8,)), dma((8,)), dma((8,)),
-            dma((nv, size_x + 2)), dma((nv, size_x + 2)),
+            dma((nv, 5)), dma((nv, 5)), dma((nv, 8)), dma((nv, 8)),
         ],
         compiler_params=pltpu.CompilerParams(collective_id=0, has_side_effects=True),
         name="smooth",

time: 42.8 us -> 39.2 us (0.916)
  Pallas kernels: 40.2 us -> 36.5 us
    pallas_call x1, Pallas kernels: 26.2 us -> 22.5 us  [body(): pl.pallas_call(functools.partial(smooth_kernel, nx, ny, nv), out_shape=(j...]
where the time goes in v3:
time: 39.2 us; the launch traced here: 39 us
  Pallas kernels  36.5 us (93%)
  local copies, waits for them, and re-layouts  1.81 us (5%)
  between operations  0.64 us (2%)
    pallas_call x1, Pallas kernels, body(): pl.pallas_call(functools.partial(smooth_kernel, nx, ny, nv), out_shape=(j...  22.5 us
    pallas_call x1, Pallas kernels, body(): pl.pallas_call(functools.partial(coarse_kernel, size_x, size_y, slots), o...  14 us
    unnamed x1, local copies, waits for them, and re-layouts  1.81 us

profile of v3, /device:TPU:1, one launch (start us, length us, event | category | flops | bytes accessed | tf_op | source)
XLA Modules:
  0.0 39.0 jit_solution(7066694915982997926)
XLA Ops:
  0.6 1.8 %copy.7 = f32[8,8,8,128]{3,0,2,1:T(8,128)} copy(f32[8,8,8,128]{3,2,1,0:T(8,128)} %param.3) | data formatting | bytes 524288 | tf_op args[0]
  2.4 22.5 %smooth.1 = (f32[2,10,10,8,128]{4,3,2,1,0:T(8,128)}, f32[10,10,1,128]{3,2,1,0:T(1,128)}, s32[10,10,1,16]{3,2,1,0:T(1,128)}) custom-call(f32[8,8,8,128]{3,2,1,0:T(8,128)} %bitcast.9, f32[8,8,1,128]{3,2,1,0:T(1,128)} %bitcast.13, s32[8,8,1,16]{3,2,1,0:T(1,128)} %bitcast.14), custom_call_target="tpu_custom_call" | custom-call | tf_op jit(solution)/shard_map/smooth/pallas_call | solution.py:492
  25.0 14.0 %coarse.1 = (f32[8,8,16,128]{3,2,1,0:T(8,128)}, f32[8,9,8,256]{3,2,1,0:T(8,128)}) custom-call(f32[2,100,8,128]{3,2,1,0:T(8,128)} %bitcast.10, f32[100,1,128]{2,1,0:T(1,128)} %bitcast.11, s32[100,1,16]{2,1,0:T(1,128)} %bitcast.12), custom_call_target="tpu_custom_call" | custom-call | tf_op jit(solution)/shard_map/coarse/pallas_call | solution.py:516

commit v4 on v3

--- a/solution.py
+++ b/solution.py
@@ -14,7 +14,9 @@
 RIDGE = 0.1
 HALO = SWEEPS
 GROUP = 8
-UNROLL = True
+BATCH = 7
+BATCH_2 = 2
+ROWS = True
 MESH = pl.DeviceIdType.MESH
 F32 = jnp.float32
 BF16 = jnp.bfloat16
@@ -62,9 +64,9 @@
 
 
 def smooth_kernel(
-    nx, ny, nv, v_ref, k_ref, c_ref, out_ref, knots_ref, spots_ref,
+    nx, ny, nv, raw_ref, k_ref, c_ref, out_ref, knots_ref, spots_ref,
     one, two, gain, wide_k, wide_c, ksend, krecv, csend, crecv, vsend, vrecv,
-    fsend, frecv, hsend, hrecv,
+    fsend, frecv, hsend, hrecv, v_ref, turn,
 ):
     size_x, size_y, vecs, depth = v_ref.shape
     wide_x, wide_y = size_x + 2 * HALO, size_y + 2 * HALO
@@ -75,6 +77,13 @@
         ok_x = jnp.logical_and(gx + mx >= 0, gx + mx < nx)
         ok_y = jnp.logical_and(gy + my >= 0, gy + my < ny)
         return jnp.logical_and(ok_x, ok_y)
+
+    turns = [
+        pltpu.make_async_copy(raw_ref.at[vec], v_ref.at[:, :, vec], turn.at[vec])
+        for vec in range(vecs)
+    ]
+    for copy in turns:
+        copy.start()
 
     barrier = pltpu.get_barrier_semaphore()
     total = jnp.int32(nv - 1)
@@ -123,8 +132,7 @@
 
         @pl.when(inside(mx, my))
         def _():
-            for kind in range(3):
-                departure(kind, no).start()
+            departure(0, no).start()
 
         @pl.when(jnp.logical_not(inside(mx, my)))
         def _():
@@ -136,6 +144,15 @@
             rim_x, rim_y = rim(mx, size_x), rim(my, size_y)
             out_ref[:, rim_x, rim_y] = jnp.zeros((nv, rim_x.size, rim_y.size, vecs, depth), F32)
 
+    for copy in turns:
+        copy.wait()
+    for kind in (1, 2):
+        for no, (mx, my) in enumerate(moves):
+
+            @pl.when(inside(mx, my))
+            def _():
+                departure(kind, no).start()
+
     for source, target, _, _ in kinds:
         target[pl.ds(HALO, size_x), pl.ds(HALO, size_y)] = source[...]
 
@@ -299,7 +316,7 @@
 
 def coarse_kernel(
     size_x, size_y, slots, f_ref, k_ref, c_ref, interp_ref, coarse_ref,
-    hot, right_s, gram_s, lh, ll, rh, rl, ch,
+    hot, right_h, right_l, gram_s, lh, ll, rh, rl, ch,
 ):
     nv, cols, vecs, depth = f_ref.shape
     wide_y = size_y + 2
@@ -323,30 +340,37 @@
     def start_of(no):
         return jnp.minimum(no * GROUP, cols - GROUP)
 
-    def gather(no, carry):
-        start = start_of(no)
-        knots = k_ref[pl.ds(start, GROUP)]
-        alive = knots > 0.0
-        inverse = jnp.where(alive, 1.0 / jnp.where(alive, knots, 1.0), 0.0)
-        field = jnp.concatenate(
-            [f_ref[half, pl.ds(start, GROUP)] * inverse for half in range(nv)], axis=1
-        ).reshape(members, depth)
-        spots = jnp.broadcast_to(
-            c_ref[pl.ds(start, GROUP)].astype(F32), (GROUP, slots, slots)
-        ).reshape(rows, slots)
-        spread = dot(jnp.where(own_lane, spots, 0.0).astype(BF16), ones, NN)
-        onehot = jnp.where(spread == lanes((rows, depth)).astype(F32), 1.0, 0.0)
-        hot[no] = onehot
-        fh, fl = split(field)
-        picked = onehot.astype(BF16)
-        cvals = jnp.where(same, dot(picked, fh, NT) + dot(picked, fl, NT), 0.0)
-        pair = split(cvals)
-        right_s[no] = dot3(pair, (fh, fl), NN)
-        gram = dot3(pair, pair, NT)
-        gram_s[no] = jnp.sum(gram.reshape(GROUP, slots, rows), axis=0)
-        return carry
-
-    lax.fori_loop(0, count, gather, 0, unroll=UNROLL)
+    def gather(batch):
+        fields, spreads = [], []
+        for no in batch:
+            start = min(no * GROUP, cols - GROUP)
+            knots = k_ref[pl.ds(start, GROUP)]
+            alive = knots > 0.0
+            inverse = jnp.where(alive, 1.0 / jnp.where(alive, knots, 1.0), 0.0)
+            field = jnp.concatenate(
+                [f_ref[half, pl.ds(start, GROUP)] * inverse for half in range(nv)], axis=1
+            ).reshape(members, depth)
+            fields.append(split(field))
+            spots = jnp.broadcast_to(
+                c_ref[pl.ds(start, GROUP)].astype(F32), (GROUP, slots, slots)
+            ).reshape(rows, slots)
+            spreads.append(dot(jnp.where(own_lane, spots, 0.0).astype(BF16), ones, NN))
+        pairs = []
+        for no, spread, (high, low) in zip(batch, spreads, fields):
+            onehot = jnp.where(spread == lanes((rows, depth)).astype(F32), 1.0, 0.0).astype(BF16)
+            hot[no] = onehot
+            pairs.append(dot(onehot, high, NT) + dot(onehot, low, NT))
+        pairs = [split(jnp.where(same, cvals, 0.0)) for cvals in pairs]
+        grams = [dot3(pair, pair, NT) for pair in pairs]
+        rights = [dot3(pair, field, NN) for pair, field in zip(pairs, fields)]
+        for no, gram, right in zip(batch, grams, rights):
+            gram_s[no] = jnp.sum(gram.reshape(GROUP, slots, rows), axis=0)
+            high, low = split(right)
+            right_h[no] = high
+            right_l[no] = low
+
+    for first in range(0, count, BATCH):
+        gather(range(first, min(first + BATCH, count)))
 
     shape = (count, slots, rows)
     lane = lanes(shape) % slots
@@ -375,29 +399,36 @@
         )
     gram_s[...] = system
 
-    def weigh(no, carry):
-        start = start_of(no)
-        inverse = jnp.where(
-            same_slots,
-            jnp.broadcast_to(gram_s[no][None], (GROUP, slots, rows)).reshape(rows, rows),
-            0.0,
-        )
-        weights = dot3(split(inverse), split(right_s[no]), NN).reshape(GROUP, slots, depth)
-        onehot = hot[no].reshape(GROUP, slots, depth)
-        crow = jnp.sum(onehot, axis=1, keepdims=True)
-        value = weights * (1.0 - crow) + onehot
-        hot_cols = pl.ds(start, GROUP)
-        ch[hot_cols] = value
-        left = value * k_ref[hot_cols]
-        high, low = split(left.reshape(rows, depth))
-        lh[hot_cols] = high.reshape(GROUP, slots, depth)
-        ll[hot_cols] = low.reshape(GROUP, slots, depth)
-        high, low = split(smear_z(left.reshape(rows, depth)))
-        rh[hot_cols] = high.reshape(GROUP, slots, depth)
-        rl[hot_cols] = low.reshape(GROUP, slots, depth)
-        return carry
-
-    lax.fori_loop(0, count, weigh, 0, unroll=UNROLL)
+    def weigh(batch):
+        inverses = [
+            split(
+                jnp.where(
+                    same_slots,
+                    jnp.broadcast_to(gram_s[no][None], (GROUP, slots, rows)).reshape(rows, rows),
+                    0.0,
+                )
+            )
+            for no in batch
+        ]
+        solved = [
+            dot3(inverse, (right_h[no], right_l[no]), NN) for no, inverse in zip(batch, inverses)
+        ]
+        for no, weights in zip(batch, solved):
+            here = pl.ds(min(no * GROUP, cols - GROUP), GROUP)
+            onehot = hot[no].astype(F32).reshape(GROUP, slots, depth)
+            crow = jnp.sum(onehot, axis=1, keepdims=True)
+            value = weights.reshape(GROUP, slots, depth) * (1.0 - crow) + onehot
+            ch[here] = value
+            left = value * k_ref[here]
+            high, low = split(left)
+            lh[here] = high
+            ll[here] = low
+            high, low = split(smear_z(left.reshape(rows, depth)))
+            rh[here] = high.reshape(GROUP, slots, depth)
+            rl[here] = low.reshape(GROUP, slots, depth)
+
+    for first in range(0, count, BATCH_2):
+        weigh(range(first, min(first + BATCH_2, count)))
 
     half = GROUP * slots
     groups = slots * slots // half
@@ -478,13 +509,12 @@
                     )
         return carry
 
-    lax.fori_loop(0, size_x, galerkin, 0)
+    lax.fori_loop(0, size_x, galerkin, 0, unroll=ROWS)
 
 
 def body(nx, ny, nv, vectors, conductivity, c_points):
     vecs, size_x, size_y, depth = vectors.shape
     slots = c_points.shape[-1]
-    turned = jnp.transpose(vectors, (1, 2, 0, 3))
     wide_x, wide_y = size_x + 2 * HALO, size_y + 2 * HALO
     cols = (size_x + 2) * (size_y + 2)
     vmem = pl.BlockSpec(memory_space=pltpu.VMEM)
@@ -496,7 +526,7 @@
             jax.ShapeDtypeStruct((size_x + 2, size_y + 2, 1, depth), F32),
             jax.ShapeDtypeStruct((size_x + 2, size_y + 2, 1, slots), jnp.int32),
         ),
-        in_specs=[vmem] * 3,
+        in_specs=[pl.BlockSpec(memory_space=pl.ANY), vmem, vmem],
         out_specs=(vmem,) * 3,
         scratch_shapes=[
             pltpu.VMEM((wide_x, wide_y, vecs, depth), F32),
@@ -506,10 +536,11 @@
             pltpu.VMEM((wide_x, wide_y, 1, slots), jnp.int32),
             dma((8,)), dma((8,)), dma((8,)), dma((8,)), dma((8,)), dma((8,)),
             dma((nv, 5)), dma((nv, 5)), dma((nv, 8)), dma((nv, 8)),
+            pltpu.VMEM((size_x, size_y, vecs, depth), F32), dma((vecs,)),
         ],
         compiler_params=pltpu.CompilerParams(collective_id=0, has_side_effects=True),
         name="smooth",
-    )(turned, conductivity[:, :, None, :], c_points[:, :, None, :])
+    )(vectors, conductivity[:, :, None, :], c_points[:, :, None, :])
     count = -(-cols // GROUP)
     rows = GROUP * slots
     more = cols + 2 * GROUP
@@ -522,8 +553,9 @@
         in_specs=[vmem] * 3,
         out_specs=(vmem, vmem),
         scratch_shapes=[
-            pltpu.VMEM((count, rows, depth), F32),
-            pltpu.VMEM((count, rows, depth), F32),
+            pltpu.VMEM((count, rows, depth), BF16),
+            pltpu.VMEM((count, rows, depth), BF16),
+            pltpu.VMEM((count, rows, depth), BF16),
             pltpu.VMEM((count, slots, rows), F32),
             pltpu.VMEM((more, slots, depth), BF16),
             pltpu.VMEM((more, slots, depth), BF16),

time: 39.2 us -> 34.5 us (0.88)
  Pallas kernels: 36.5 us -> 33.6 us
  local copies, waits for them, and re-layouts: 1.81 us -> 0 us
    pallas_call x1, Pallas kernels: 14 us -> 9.2 us  [body(): pl.pallas_call(functools.partial(coarse_kernel, size_x, size_y, slots), o...]
    pallas_call x1, Pallas kernels: 22.5 us -> 24.4 us  [body(): pl.pallas_call(functools.partial(smooth_kernel, nx, ny, nv), out_shape=(j...]
    unnamed x1 -> x0, local copies, waits for them, and re-layouts: 1.81 us -> none
where the time goes in v4:
time: 34.5 us; the launch traced here: 34.3 us
  Pallas kernels  33.6 us (97%)
  between operations  0.64 us (2%)
    pallas_call x1, Pallas kernels, body(): pl.pallas_call(functools.partial(smooth_kernel, nx, ny, nv), out_shape=(j...  24.4 us
    pallas_call x1, Pallas kernels, body(): pl.pallas_call(functools.partial(coarse_kernel, size_x, size_y, slots), o...  9.2 us

profile of v4, /device:TPU:1, one launch (start us, length us, event | category | flops | bytes accessed | tf_op | source)
XLA Modules:
  0.0 34.3 jit_solution(5513222770522765686)
XLA Ops:
  0.6 24.4 %smooth.1 = (f32[2,10,10,8,128]{4,3,2,1,0:T(8,128)}, f32[10,10,1,128]{3,2,1,0:T(1,128)}, s32[10,10,1,16]{3,2,1,0:T(1,128)}) custom-call(f32[8,8,8,128]{3,2,1,0:T(8,128)} %raw_ref.1, f32[8,8,1,128]{3,2,1,0:T(1,128)} %bitcast.9, s32[8,8,1,16]{3,2,1,0:T(1,128)} %bitcast.10), custom_call_target="tpu_custom_call" | custom-call | tf_op jit(solution)/shard_map/smooth/pallas_call | solution.py:522
  25.1 9.2 %coarse.1 = (f32[8,8,16,128]{3,2,1,0:T(8,128)}, f32[8,9,8,256]{3,2,1,0:T(8,128)}) custom-call(f32[2,100,8,128]{3,2,1,0:T(8,128)} %bitcast.6, f32[100,1,128]{2,1,0:T(1,128)} %bitcast.7, s32[100,1,16]{2,1,0:T(1,128)} %bitcast.8), custom_call_target="tpu_custom_call" | custom-call | tf_op jit(solution)/shard_map/coarse/pallas_call | solution.py:547

commit v5 on v4

--- a/solution.py
+++ b/solution.py
@@ -14,7 +14,7 @@
 RIDGE = 0.1
 HALO = SWEEPS
 GROUP = 8
-BATCH = 7
+BATCH = 13
 BATCH_2 = 2
 ROWS = True
 MESH = pl.DeviceIdType.MESH
@@ -178,21 +178,20 @@
             gain[row, col] = jnp.broadcast_to(value, (vecs, depth))
         return carry
 
-    lax.fori_loop(1, wide_x - 1, gains, 0)
+    lax.fori_loop(1, wide_x - 1, gains, 0, unroll=2)
 
     for no, (mx, my) in enumerate(moves):
 
         @pl.when(inside(mx, my))
         def _():
             arrival(1, no).wait_recv()
-            arrival(2, no).wait_recv()
 
     def scale(row, carry):
         for col in range(wide_y):
             one[row, col] = one[row, col] * jnp.broadcast_to(pick_k(wide_k, row, col), (vecs, depth))
         return carry
 
-    lax.fori_loop(0, wide_x, scale, 0)
+    lax.fori_loop(0, wide_x, scale, 0, unroll=2)
 
     def relaxed(ref, row, first, last):
         around = smear_row(ref, row, first, last, pick_u)
@@ -210,7 +209,7 @@
                 target[row, sweep + no] = value
             return carry
 
-        lax.fori_loop(sweep, wide_x - sweep, step, 0)
+        lax.fori_loop(sweep, wide_x - sweep, step, 0, unroll=2)
         source, target = target, source
 
     def last_sweep(row, carry):
@@ -218,7 +217,7 @@
             out_ref[gv, row - SWEEPS + 1, no + 1] = value
         return carry
 
-    lax.fori_loop(SWEEPS, wide_x - SWEEPS, last_sweep, 0)
+    lax.fori_loop(SWEEPS, wide_x - SWEEPS, last_sweep, 0, unroll=2)
 
     pieces = (
         (pl.ds(1, 1), pl.ds(1, size_y)),
@@ -276,6 +275,12 @@
             @pl.when(inside(mx, my))
             def _():
                 rim_departure(step, half, no).start()
+
+    for no, (mx, my) in enumerate(moves):
+
+        @pl.when(inside(mx, my))
+        def _():
+            arrival(2, no).wait_recv()
 
     rim_x, rim_y = pl.ds(HALO - 1, size_x + 2), pl.ds(HALO - 1, size_y + 2)
     knots_ref[...] = wide_k[rim_x, rim_y]

time: 34.5 us -> 31.1 us (0.901)
  Pallas kernels: 33.6 us -> 30.2 us
    pallas_call x1, Pallas kernels: 24.4 us -> 21.2 us  [body(): pl.pallas_call(functools.partial(smooth_kernel, nx, ny, nv), out_shape=(j...]
where the time goes in v5:
time: 31.1 us; the launch traced here: 30.9 us
  Pallas kernels  30.2 us (97%)
  between operations  0.64 us (2%)
    pallas_call x1, Pallas kernels, body(): pl.pallas_call(functools.partial(smooth_kernel, nx, ny, nv), out_shape=(j...  21.2 us
    pallas_call x1, Pallas kernels, body(): pl.pallas_call(functools.partial(coarse_kernel, size_x, size_y, slots), o...  9.02 us

profile of v5, /device:TPU:1, one launch (start us, length us, event | category | flops | bytes accessed | tf_op | source)
XLA Modules:
  0.0 30.9 jit_solution(4322093481290197330)
XLA Ops:
  0.6 21.2 %smooth.1 = (f32[2,10,10,8,128]{4,3,2,1,0:T(8,128)}, f32[10,10,1,128]{3,2,1,0:T(1,128)}, s32[10,10,1,16]{3,2,1,0:T(1,128)}) custom-call(f32[8,8,8,128]{3,2,1,0:T(8,128)} %raw_ref.1, f32[8,8,1,128]{3,2,1,0:T(1,128)} %bitcast.9, s32[8,8,1,16]{3,2,1,0:T(1,128)} %bitcast.10), custom_call_target="tpu_custom_call" | custom-call | tf_op jit(solution)/shard_map/smooth/pallas_call | solution.py:527
  21.8 9.0 %coarse.1 = (f32[8,8,16,128]{3,2,1,0:T(8,128)}, f32[8,9,8,256]{3,2,1,0:T(8,128)}) custom-call(f32[2,100,8,128]{3,2,1,0:T(8,128)} %bitcast.6, f32[100,1,128]{2,1,0:T(1,128)} %bitcast.7, s32[100,1,16]{2,1,0:T(1,128)} %bitcast.8), custom_call_target="tpu_custom_call" | custom-call | tf_op jit(solution)/shard_map/coarse/pallas_call | solution.py:552

commit v6 on v5

--- a/solution.py
+++ b/solution.py
@@ -43,18 +43,18 @@
     ]
 
 
-def span(move, size):
+def span(move, size, deep):
     if move == 0:
         return pl.ds(0, size), pl.ds(HALO, size)
     if move > 0:
-        return pl.ds(size - HALO, HALO), pl.ds(0, HALO)
-    return pl.ds(0, HALO), pl.ds(size + HALO, HALO)
-
-
-def hole(move, size):
+        return pl.ds(size - deep, deep), pl.ds(HALO - deep, deep)
+    return pl.ds(0, deep), pl.ds(size + HALO, deep)
+
+
+def hole(move, size, deep=HALO):
     if move == 0:
         return pl.ds(HALO, size)
-    return pl.ds(size + HALO, HALO) if move > 0 else pl.ds(0, HALO)
+    return pl.ds(size + HALO, deep) if move > 0 else pl.ds(HALO - deep, deep)
 
 
 def rim(move, size):
@@ -107,11 +107,13 @@
         (k_ref, wide_k, ksend, krecv), (v_ref, one, vsend, vrecv), (c_ref, wide_c, csend, crecv),
     )
 
+    depths = (HALO, HALO, 1)
+
     def departure(kind, no):
         mx, my = moves[no]
         source, target, send, recv = kinds[kind]
-        from_x, to_x = span(mx, size_x)
-        from_y, to_y = span(my, size_y)
+        from_x, to_x = span(mx, size_x, depths[kind])
+        from_y, to_y = span(my, size_y, depths[kind])
         return pltpu.make_async_remote_copy(
             src_ref=source.at[from_x, from_y], dst_ref=target.at[to_x, to_y],
             send_sem=send.at[no], recv_sem=recv.at[no],
@@ -122,7 +124,7 @@
         mx, my = moves[no]
         other = moves.index((-mx, -my))
         _, target, send, recv = kinds[kind]
-        place = target.at[hole(mx, size_x), hole(my, size_y)]
+        place = target.at[hole(mx, size_x, depths[kind]), hole(my, size_y, depths[kind])]
         return pltpu.make_async_remote_copy(
             src_ref=place, dst_ref=place, send_sem=send.at[other], recv_sem=recv.at[other],
             device_id=(gx + mx, gy + my, gv), device_id_type=MESH,

time: 31.1 us -> 31.1 us (level)
  no operation moved by 1% of the time
where the time goes in v6:
time: 31.1 us; the launch traced here: 30.9 us
  Pallas kernels  30.3 us (97%)
  between operations  0.64 us (2%)
    pallas_call x1, Pallas kernels, body(): pl.pallas_call(functools.partial(smooth_kernel, nx, ny, nv), out_shape=(j...  21.2 us
    pallas_call x1, Pallas kernels, body(): pl.pallas_call(functools.partial(coarse_kernel, size_x, size_y, slots), o...  9.03 us

profile of v6, /device:TPU:1, one launch (start us, length us, event | category | flops | bytes accessed | tf_op | source)
XLA Modules:
  0.0 30.9 jit_solution(16930016650898152894)
XLA Ops:
  0.6 21.2 %smooth.1 = (f32[2,10,10,8,128]{4,3,2,1,0:T(8,128)}, f32[10,10,1,128]{3,2,1,0:T(1,128)}, s32[10,10,1,16]{3,2,1,0:T(1,128)}) custom-call(f32[8,8,8,128]{3,2,1,0:T(8,128)} %raw_ref.1, f32[8,8,1,128]{3,2,1,0:T(1,128)} %bitcast.9, s32[8,8,1,16]{3,2,1,0:T(1,128)} %bitcast.10), custom_call_target="tpu_custom_call" | custom-call | tf_op jit(solution)/shard_map/smooth/pallas_call | solution.py:529
  21.9 9.0 %coarse.1 = (f32[8,8,16,128]{3,2,1,0:T(8,128)}, f32[8,9,8,256]{3,2,1,0:T(8,128)}) custom-call(f32[2,100,8,128]{3,2,1,0:T(8,128)} %bitcast.6, f32[100,1,128]{2,1,0:T(1,128)} %bitcast.7, s32[100,1,16]{2,1,0:T(1,128)} %bitcast.8), custom_call_target="tpu_custom_call" | custom-call | tf_op jit(solution)/shard_map/coarse/pallas_call | solution.py:554
